TPU v7x, 32 devices: a whole 2x2x4 slice. The times are simulated.
32 devices in a mesh: wide: 8 (over z, x), narrow: 4 (over y, core).
Axes of the slice: x: 2, y: 2, z: 4, core: 2. Of those that a mesh axis runs over, the one named last changes fastest.
Arguments:
- words_first: bfloat16 [32, 512, 768], P(('wide', 'narrow')), may hold values from -6 to 6
- entities_first: bfloat16 [32, 128, 768], P(('wide', 'narrow')), may hold values from -6 to 6
- positions_first: int32 [32, 128], P(('wide', 'narrow')), may hold values from 0 to 511
- entity_slots_first: int32 [32, 12], P(('wide', 'narrow')), may hold values from -1 to 127, as said below
- entity_labels_first: int32 [32, 12], P(('wide', 'narrow')), may hold values from 0 to 32767
- words_second: bfloat16 [32, 512, 768], P(('wide', 'narrow')), may hold values from -6 to 6
- entities_second: bfloat16 [32, 128, 768], P(('wide', 'narrow')), may hold values from -6 to 6
- positions_second: int32 [32, 128], P(('wide', 'narrow')), may hold values from 0 to 511
- word_slots_second: int32 [32, 64], P(('wide', 'narrow')), may hold values from -1 to 511, as said below
- word_labels_second: int32 [32, 64], P(('wide', 'narrow')), may hold values from 0 to 4095
- entity_slots_second: int32 [32, 12], P(('wide', 'narrow')), may hold values from -1 to 127, as said below
- entity_labels_second: int32 [32, 12], P(('wide', 'narrow')), may hold values from 0 to 32767
- query_word_word: bfloat16 [768, 768], P('narrow'), may hold values from -0.21875 to 0.21875
- query_word_entity: bfloat16 [768, 768], P('narrow'), may hold values from -0.21875 to 0.21875
- query_entity_word: bfloat16 [768, 768], P('narrow'), may hold values from -0.21875 to 0.21875
- query_entity_entity: bfloat16 [768, 768], P('narrow'), may hold values from -0.21875 to 0.21875
- key_weight: bfloat16 [768, 768], P('narrow'), may hold values from -0.21875 to 0.21875
- value_weight: bfloat16 [768, 768], P('narrow'), may hold values from -0.21875 to 0.21875
- output_weight: bfloat16 [768, 768], P('narrow'), may hold values from -3 to 3
- attention_gain: bfloat16 [768], P('narrow'), may hold values from 0.5 to 1.5
- attention_bias: bfloat16 [768], P('narrow'), may hold values from -2 to 2
- up_weight: bfloat16 [768, 3072], P('narrow'), may hold values from -0.21875 to 0.21875
- down_weight: bfloat16 [3072, 768], P('narrow'), may hold values from -0.109375 to 0.109375
- feedforward_gain: bfloat16 [768], P('narrow'), may hold values from 0.5 to 1.5
- feedforward_bias: bfloat16 [768], P('narrow'), may hold values from -2 to 2
- word_table: bfloat16 [4096, 768], P(('wide', 'narrow')), may hold values from -0.4375 to 0.4375
- entity_dense: bfloat16 [768, 256], P('narrow'), may hold values from -0.21875 to 0.21875
- entity_table: bfloat16 [32768, 256], P(('wide', 'narrow')), may hold values from -1 to 1
- position_table: bfloat16 [512, 768], P('narrow'), may hold values from -3 to 3
Outputs:
- entity_word_grad_first: float32 [768, 768], P('narrow')
- entity_entity_grad_first: float32 [768, 768], P('narrow')
- loss_second: float32 [], replicated
- words_grad: bfloat16 [32, 512, 768], P(('wide', 'narrow'))
- entities_grad: bfloat16 [32, 128, 768], P(('wide', 'narrow'))
- query_word_word_grad: float32 [768, 768], P('narrow')
- query_word_entity_grad: float32 [768, 768], P('narrow')
- query_entity_word_grad: float32 [768, 768], P('narrow')
- query_entity_entity_grad: float32 [768, 768], P('narrow')
- key_weight_grad: float32 [768, 768], P('narrow')
- value_weight_grad: float32 [768, 768], P('narrow')
- output_weight_grad: float32 [768, 768], P('narrow')
- attention_gain_grad: float32 [768], P('narrow')
- attention_bias_grad: float32 [768], P('narrow')
- up_weight_grad: float32 [768, 3072], P('narrow')
- down_weight_grad: float32 [3072, 768], P('narrow')
- feedforward_gain_grad: float32 [768], P('narrow')
- feedforward_bias_grad: float32 [768], P('narrow')
- word_table_grad: float32 [4096, 768], P(('wide', 'narrow'))
- entity_dense_grad: float32 [768, 256], P('narrow')
- entity_table_grad: float32 [32768, 256], P(('wide', 'narrow'))
- position_table_grad: float32 [512, 768], P('narrow')
Inputs may be any that keep to these rules, and one draw needn't show every extreme that they name: `word_slots_second`: in each row the used slots come first and hold distinct word positions, the rest hold -1; some row of the batch uses all 64 slots. `entity_slots_first`: in each row the used slots come first and hold distinct entity positions, the rest hold -1; some row of the batch uses all 12 slots. `entity_slots_second`: in each row the used slots come first and hold distinct entity positions, the rest hold -1; some row of the batch uses all 12 slots.
All inputs are finite; a program needn't handle non-finite values.
Results may differ from a plain program's by a relative error of at most 0.025.
The roundings to bfloat16 on the way count: a program that leaves them out, or rounds other values in their place, can miss the bound.
Values may be sent and summed in bfloat16 or wider, within the bound.
No kernel may reach another device: no remote copies, remote signals or barrier semaphores. Data moves between devices by JAX's collectives and lax.ppermute only.
A program may use at most 576 MiB of HBM per device.

v0:
```python
import jax
import jax.numpy as jnp
from jax import lax
from jax.sharding import PartitionSpec as P

HEADS = 12
HD = 64


EPS = 1e-05
HALF_ROOT = 0.7071067811865476
NORMAL_PEAK = 0.3989422804014327


def combined_all(value, axis, join):
    pieces = jax.tree.map(lambda part: lax.all_gather(part, axis), value)
    head = jax.tree.map(lambda part: part[0], pieces)
    tail = jax.tree.map(lambda part: part[1:], pieces)
    subtotal, _ = lax.scan(lambda subtotal, piece: (join(subtotal, piece), None), head, tail)
    return subtotal


def matmul(inputs, weight):
    return jnp.einsum("rld,de->rle", inputs, weight, preferred_element_type=jnp.float32)


def matmul_back(grads, weight):
    return jnp.einsum("rle,de->rld", grads, weight, preferred_element_type=jnp.float32)


def weight_grad(inputs, grads):
    return jnp.einsum("rld,rle->de", inputs, grads, preferred_element_type=jnp.float32)


def gather_rows(values, position):
    return jax.vmap(lambda table, picked: table[picked])(values, position)


def spread_rows(grads, position, length):
    onehot = (position[:, :, None] == jnp.arange(length)[None, None, :]).astype(jnp.float32)
    return jnp.einsum("rsn,rsd->rnd", onehot, grads, precision=lax.Precision.HIGHEST)


def head_groups():
    return 2


def to_groups(values):
    rows, count = (values.shape[0], values.shape[1])
    groups = head_groups()
    shaped = values.reshape(rows, count, groups, HEADS // groups, HD)
    return jnp.transpose(shaped, (0, 2, 1, 3, 4)).reshape(rows * groups, count, HEADS // groups, HD)


def from_groups(values, rows):
    groups = head_groups()
    count = values.shape[1]
    shaped = values.reshape(rows, groups, count, HEADS // groups, HD)
    return jnp.transpose(shaped, (0, 2, 1, 3, 4)).reshape(rows, count, HEADS * HD)


def norm_forward(resid, gain, bias):
    average = jnp.mean(resid, axis=-1, keepdims=True)
    centered = resid - average
    inverse = lax.rsqrt(jnp.mean(centered * centered, axis=-1, keepdims=True) + EPS)
    normal = centered * inverse
    return (normal * gain.astype(jnp.float32) + bias.astype(jnp.float32), normal, inverse)


def norm_backward(grads, normal, inverse, gain):
    scaled = grads * gain.astype(jnp.float32)
    centered = scaled - jnp.mean(scaled, axis=-1, keepdims=True)
    resid_grad = inverse * (centered - normal * jnp.mean(scaled * normal, axis=-1, keepdims=True))
    return (resid_grad, jnp.sum(grads * normal, axis=(0, 1)), jnp.sum(grads, axis=(0, 1)))


def score_block(first, second, keys, split):
    scores = jnp.concatenate(
        [
            jnp.einsum("qhd,khd->hqk", first, keys[:split], preferred_element_type=jnp.float32),
            jnp.einsum("qhd,khd->hqk", second, keys[split:], preferred_element_type=jnp.float32),
        ],
        axis=-1,
    )
    return scores * HD ** (-0.5)


def attention_forward(first, second, keys, values, split):
    scores = score_block(first, second, keys, split)
    top = jnp.max(scores, axis=-1, keepdims=True)
    expo = jnp.exp(scores - top)
    total = jnp.sum(expo, axis=-1, keepdims=True)
    probs_low = (expo / total).astype(jnp.bfloat16)
    context = jnp.einsum("hqk,khd->qhd", probs_low, values, preferred_element_type=jnp.float32)
    return (context.astype(jnp.bfloat16), (top + jnp.log(total))[..., 0])


def attention_backward(first, second, keys, values, lse, context_grad, split, with_keys):
    scale = HD ** (-0.5)
    scores = score_block(first, second, keys, split)
    probs = jnp.exp(scores - lse[..., None])
    probs_grad = jnp.einsum(
        "qhd,khd->hqk", context_grad, values, preferred_element_type=jnp.float32
    )
    scores_grad = (
        probs * (probs_grad - jnp.sum(probs * probs_grad, axis=-1, keepdims=True))
    ).astype(jnp.bfloat16)
    first_grad = (
        jnp.einsum(
            "hqk,khd->qhd",
            scores_grad[..., :split],
            keys[:split],
            preferred_element_type=jnp.float32,
        )
        * scale
    )
    second_grad = (
        jnp.einsum(
            "hqk,khd->qhd",
            scores_grad[..., split:],
            keys[split:],
            preferred_element_type=jnp.float32,
        )
        * scale
    )
    if not with_keys:
        return (first_grad, second_grad)
    keys_grad = (
        jnp.concatenate(
            [
                jnp.einsum(
                    "hqk,qhd->khd",
                    scores_grad[..., :split],
                    first,
                    preferred_element_type=jnp.float32,
                ),
                jnp.einsum(
                    "hqk,qhd->khd",
                    scores_grad[..., split:],
                    second,
                    preferred_element_type=jnp.float32,
                ),
            ],
            axis=0,
        )
        * scale
    )
    values_grad = jnp.einsum(
        "hqk,qhd->khd", probs.astype(jnp.bfloat16), context_grad, preferred_element_type=jnp.float32
    )
    return (first_grad, second_grad, keys_grad, values_grad)


def build_tokens(words, entities, positions, full_position):
    nearby = full_position[positions]
    tokens = jnp.concatenate(
        [words.astype(jnp.float32), entities.astype(jnp.float32) + nearby.astype(jnp.float32)],
        axis=1,
    )
    return (tokens, tokens.astype(jnp.bfloat16))


def tail_forward(resid_one, layer):
    gain_one, bias_one, full_up, full_down, gain_two, bias_two = layer
    hidden_one, normal_one, inverse_one = norm_forward(resid_one, gain_one, bias_one)
    hidden_low = hidden_one.astype(jnp.bfloat16)
    up = matmul(hidden_low, full_up)
    act_low = (0.5 * up * (1.0 + lax.erf(up * HALF_ROOT))).astype(jnp.bfloat16)
    hidden_two, normal_two, inverse_two = norm_forward(
        hidden_one + matmul(act_low, full_down), gain_two, bias_two
    )
    return (hidden_two, (normal_one, inverse_one, hidden_low, up, act_low, normal_two, inverse_two))


def tail_backward(hidden_grad, saved, layer, need_weights):
    gain_one, bias_one, full_up, full_down, gain_two, bias_two = layer
    normal_one, inverse_one, hidden_low, up, act_low, normal_two, inverse_two = saved
    resid_two_grad, gain_two_grad, bias_two_grad = norm_backward(
        hidden_grad, normal_two, inverse_two, gain_two
    )
    ffn_low = resid_two_grad.astype(jnp.bfloat16)
    act_grad = matmul_back(ffn_low, full_down)
    slope = 0.5 * (1.0 + lax.erf(up * HALF_ROOT)) + up * jnp.exp(-0.5 * up * up) * NORMAL_PEAK
    up_low = (act_grad * slope).astype(jnp.bfloat16)
    hidden_one_grad = resid_two_grad + matmul_back(up_low, full_up)
    resid_one_grad, gain_one_grad, bias_one_grad = norm_backward(
        hidden_one_grad, normal_one, inverse_one, gain_one
    )
    if not need_weights:
        return (resid_one_grad, ())
    down_grad = weight_grad(act_low, ffn_low)
    up_grad = weight_grad(hidden_low, up_low)
    return (
        resid_one_grad,
        (gain_one_grad, bias_one_grad, up_grad, down_grad, gain_two_grad, bias_two_grad),
    )


def entity_map(hidden_entities, slots, full_dense):
    picked = gather_rows(hidden_entities, jnp.maximum(slots, 0)).astype(jnp.bfloat16)
    mapped = jnp.einsum(
        "rsd,de->rse", picked, full_dense, preferred_element_type=jnp.float32
    ).astype(jnp.bfloat16)
    return (picked, mapped)


def entity_back(mapped_grad, picked, slots, full_dense, length, need_dense):
    picked_grad = jnp.einsum(
        "rse,de->rsd", mapped_grad, full_dense, preferred_element_type=jnp.float32
    )
    rows_grad = spread_rows(picked_grad, jnp.maximum(slots, 0), length)
    if not need_dense:
        return (rows_grad, None)
    return (
        rows_grad,
        jnp.einsum("rsd,rse->de", picked, mapped_grad, preferred_element_type=jnp.float32),
    )


def vocab_stats(rows, tags, table, ids):
    logits = jnp.einsum("gd,vd->gv", rows, table, preferred_element_type=jnp.float32)
    hits = tags[:, None] == ids[None, :]
    row_top = jnp.max(logits, axis=-1)
    row_total = jnp.sum(jnp.exp(logits - row_top[:, None]), axis=-1)
    row_label = jnp.sum(jnp.where(hits, logits, 0.0), axis=-1)
    return (logits, hits, (row_top, row_total, row_label))


def join_stats(first_part, second_part):
    larger = jnp.maximum(first_part[0], second_part[0])
    joined = first_part[1] * jnp.exp(first_part[0] - larger) + second_part[1] * jnp.exp(
        second_part[0] - larger
    )
    return (larger, joined, first_part[2] + second_part[2])


def join_three(first_part, second_part):
    return (
        join_stats(first_part[0:3], second_part[0:3])
        + join_stats(first_part[3:6], second_part[3:6])
        + join_stats(first_part[6:9], second_part[6:9])
    )


def vocab_grad(logits, hits, merged, tags, scale):
    norm = merged[0] + jnp.log(merged[1])
    valid = (tags >= 0).astype(jnp.float32)
    logit_grad = (
        (jnp.exp(logits - norm[:, None]) - hits.astype(jnp.float32)) * (valid * scale)[:, None]
    ).astype(jnp.bfloat16)
    return (logit_grad, (norm - merged[2]) * valid)


def tagged(slots, labels):
    return jnp.where(slots >= 0, labels, -1).reshape(-1)


def body(
    words_first,
    entities_first,
    positions_first,
    entity_slots_first,
    entity_labels_first,
    words_second,
    entities_second,
    positions_second,
    word_slots_second,
    word_labels_second,
    entity_slots_second,
    entity_labels_second,
    query_word_word,
    query_word_entity,
    query_entity_word,
    query_entity_entity,
    key_weight,
    value_weight,
    output_weight,
    attention_gain,
    attention_bias,
    up_weight,
    down_weight,
    feedforward_gain,
    feedforward_bias,
    word_table,
    entity_dense,
    entity_table,
    position_table,
):
    row_count = words_second.shape[0]
    split = words_second.shape[1]
    width = words_second.shape[2]
    ent_count = entities_second.shape[1]
    length = split + ent_count
    (
        full_ww,
        full_we,
        full_ew,
        full_ee,
        full_key,
        full_value,
        full_output,
        gain_one,
        bias_one,
        full_up,
        full_down,
        gain_two,
        bias_two,
        full_dense,
        full_position,
    ) = (
        lax.all_gather(query_word_word, "narrow", axis=0, tiled=True),
        lax.all_gather(query_word_entity, "narrow", axis=0, tiled=True),
        lax.all_gather(query_entity_word, "narrow", axis=0, tiled=True),
        lax.all_gather(query_entity_entity, "narrow", axis=0, tiled=True),
        lax.all_gather(key_weight, "narrow", axis=0, tiled=True),
        lax.all_gather(value_weight, "narrow", axis=0, tiled=True),
        lax.all_gather(output_weight, "narrow", axis=0, tiled=True),
        lax.all_gather(attention_gain, "narrow", axis=0, tiled=True),
        lax.all_gather(attention_bias, "narrow", axis=0, tiled=True),
        lax.all_gather(up_weight, "narrow", axis=0, tiled=True),
        lax.all_gather(down_weight, "narrow", axis=0, tiled=True),
        lax.all_gather(feedforward_gain, "narrow", axis=0, tiled=True),
        lax.all_gather(feedforward_bias, "narrow", axis=0, tiled=True),
        lax.all_gather(entity_dense, "narrow", axis=0, tiled=True),
        lax.all_gather(position_table, "narrow", axis=0, tiled=True),
    )
    layer = (gain_one, bias_one, full_up, full_down, gain_two, bias_two)
    ent_width = full_dense.shape[1]
    tokens_one, low_one = build_tokens(words_first, entities_first, positions_first, full_position)
    entity_one = low_one[:, split:]
    keys_one = to_groups(
        matmul(low_one, full_key).astype(jnp.bfloat16).reshape(row_count, length, HEADS, HD)
    )
    values_one = to_groups(
        matmul(low_one, full_value).astype(jnp.bfloat16).reshape(row_count, length, HEADS, HD)
    )
    first_one = to_groups(
        matmul(entity_one, full_ew).astype(jnp.bfloat16).reshape(row_count, ent_count, HEADS, HD)
    )
    second_one = to_groups(
        matmul(entity_one, full_ee).astype(jnp.bfloat16).reshape(row_count, ent_count, HEADS, HD)
    )
    context_one, lse_one = lax.map(
        lambda part: attention_forward(part[0], part[1], part[2], part[3], split),
        (first_one, second_one, keys_one, values_one),
    )
    context_one_low = from_groups(context_one, row_count)
    hidden_one, saved_one = tail_forward(
        tokens_one[:, split:] + matmul(context_one_low, full_output), layer
    )
    picked_one, mapped_one = entity_map(hidden_one, entity_slots_first, full_dense)
    tokens_two, low_two = build_tokens(
        words_second, entities_second, positions_second, full_position
    )
    word_low = low_two[:, :split]
    entity_low = low_two[:, split:]
    first_two = to_groups(
        jnp.concatenate([matmul(word_low, full_ww), matmul(entity_low, full_ew)], axis=1)
        .astype(jnp.bfloat16)
        .reshape(row_count, length, HEADS, HD)
    )
    second_two = to_groups(
        jnp.concatenate([matmul(word_low, full_we), matmul(entity_low, full_ee)], axis=1)
        .astype(jnp.bfloat16)
        .reshape(row_count, length, HEADS, HD)
    )
    keys_two = to_groups(
        matmul(low_two, full_key).astype(jnp.bfloat16).reshape(row_count, length, HEADS, HD)
    )
    values_two = to_groups(
        matmul(low_two, full_value).astype(jnp.bfloat16).reshape(row_count, length, HEADS, HD)
    )
    context_two, lse_two = lax.map(
        lambda part: attention_forward(part[0], part[1], part[2], part[3], split),
        (first_two, second_two, keys_two, values_two),
    )
    context_low = from_groups(context_two, row_count)
    hidden_two, saved_two = tail_forward(tokens_two + matmul(context_low, full_output), layer)
    picked_two, mapped_two = entity_map(hidden_two[:, split:], entity_slots_second, full_dense)
    slot_count = word_slots_second.shape[1]
    ent_slots = entity_slots_second.shape[1]
    word_position = jnp.maximum(word_slots_second, 0)
    word_rows = (
        gather_rows(hidden_two[:, :split], word_position)
        .astype(jnp.bfloat16)
        .reshape(row_count * slot_count, width)
    )
    word_tags = tagged(word_slots_second, word_labels_second)
    tags_one = tagged(entity_slots_first, entity_labels_first)
    tags_two = tagged(entity_slots_second, entity_labels_second)
    flat_one = mapped_one.reshape(row_count * ent_slots, ent_width)
    flat_two = mapped_two.reshape(row_count * ent_slots, ent_width)
    word_shard = word_table.shape[0]
    ent_shard = entity_table.shape[0]
    entity_ids = lax.axis_index(("wide", "narrow")) * ent_shard + jnp.arange(
        ent_shard, dtype=jnp.int32
    )
    all_words, all_word_tags, all_one, all_tags_one, all_two, all_tags_two = (
        lax.all_gather(word_rows, ("wide", "narrow"), axis=0, tiled=True),
        lax.all_gather(word_tags, ("wide", "narrow"), axis=0, tiled=True),
        lax.all_gather(flat_one, ("wide", "narrow"), axis=0, tiled=True),
        lax.all_gather(tags_one, ("wide", "narrow"), axis=0, tiled=True),
        lax.all_gather(flat_two, ("wide", "narrow"), axis=0, tiled=True),
        lax.all_gather(tags_two, ("wide", "narrow"), axis=0, tiled=True),
    )
    word_scale = 1.0 / jnp.sum(all_word_tags >= 0).astype(jnp.float32)
    scale_one = 1.0 / jnp.sum(all_tags_one >= 0).astype(jnp.float32)
    scale_two = 1.0 / jnp.sum(all_tags_two >= 0).astype(jnp.float32)
    word_ids = lax.axis_index(("wide", "narrow")) * word_shard + jnp.arange(
        word_shard, dtype=jnp.int32
    )
    word_logits, word_hits, word_stats = vocab_stats(all_words, all_word_tags, word_table, word_ids)
    logits_one, hits_one, stats_one = vocab_stats(all_one, all_tags_one, entity_table, entity_ids)
    logits_two, hits_two, stats_two = vocab_stats(all_two, all_tags_two, entity_table, entity_ids)
    merged = combined_all(
        (
            word_stats[0],
            word_stats[1],
            word_stats[2],
            stats_one[0],
            stats_one[1],
            stats_one[2],
            stats_two[0],
            stats_two[1],
            stats_two[2],
        ),
        ("wide", "narrow"),
        join_three,
    )
    word_grad_low, word_terms = vocab_grad(
        word_logits, word_hits, merged[0:3], all_word_tags, word_scale
    )
    grad_one_low, terms_one = vocab_grad(logits_one, hits_one, merged[3:6], all_tags_one, scale_one)
    grad_two_low, terms_two = vocab_grad(logits_two, hits_two, merged[6:9], all_tags_two, scale_two)
    table_grad = jnp.einsum(
        "gv,gd->vd", word_grad_low, all_words, preferred_element_type=jnp.float32
    )
    etable_grad = jnp.einsum("gv,ge->ve", grad_two_low, all_two, preferred_element_type=jnp.float32)
    word_rows_grad, map_grad_one, map_grad_two = (
        lax.psum_scatter(
            jnp.einsum("gv,vd->gd", word_grad_low, word_table, preferred_element_type=jnp.float32),
            ("wide", "narrow"),
            scatter_dimension=0,
            tiled=True,
        ),
        lax.psum_scatter(
            jnp.einsum("gv,ve->ge", grad_one_low, entity_table, preferred_element_type=jnp.float32),
            ("wide", "narrow"),
            scatter_dimension=0,
            tiled=True,
        ),
        lax.psum_scatter(
            jnp.einsum("gv,ve->ge", grad_two_low, entity_table, preferred_element_type=jnp.float32),
            ("wide", "narrow"),
            scatter_dimension=0,
            tiled=True,
        ),
    )
    loss_second = jnp.sum(word_terms) * word_scale + jnp.sum(terms_two) * scale_two
    map_low_one = map_grad_one.astype(jnp.bfloat16).reshape(row_count, ent_slots, ent_width)
    map_low_two = map_grad_two.astype(jnp.bfloat16).reshape(row_count, ent_slots, ent_width)
    entity_grad_one = entity_back(
        map_low_one, picked_one, entity_slots_first, full_dense, ent_count, False
    )[0]
    resid_one_grad = tail_backward(entity_grad_one, saved_one, layer, False)[0]
    context_one_grad = to_groups(
        matmul_back(resid_one_grad.astype(jnp.bfloat16), full_output)
        .astype(jnp.bfloat16)
        .reshape(row_count, ent_count, HEADS, HD)
    )
    first_one_grad, second_one_grad = lax.map(
        lambda part: attention_backward(
            part[0], part[1], part[2], part[3], part[4], part[5], split, False
        ),
        (first_one, second_one, keys_one, values_one, lse_one, context_one_grad),
    )
    ew_first = weight_grad(entity_one, from_groups(first_one_grad, row_count).astype(jnp.bfloat16))
    ee_first = weight_grad(entity_one, from_groups(second_one_grad, row_count).astype(jnp.bfloat16))
    entity_rows_grad, dense_grad = entity_back(
        map_low_two, picked_two, entity_slots_second, full_dense, ent_count, True
    )
    word_spread = spread_rows(
        word_rows_grad.reshape(row_count, slot_count, width), word_position, split
    )
    hidden_grad = jnp.concatenate([word_spread, entity_rows_grad], axis=1)
    resid_grad, tail_grads = tail_backward(hidden_grad, saved_two, layer, True)
    gain_one_grad, bias_one_grad, up_grad, down_grad, gain_two_grad, bias_two_grad = tail_grads
    attended_low = resid_grad.astype(jnp.bfloat16)
    output_grad = weight_grad(context_low, attended_low)
    context_grad = to_groups(
        matmul_back(attended_low, full_output)
        .astype(jnp.bfloat16)
        .reshape(row_count, length, HEADS, HD)
    )
    first_grad, second_grad, keys_grad, values_grad = lax.map(
        lambda part: attention_backward(
            part[0], part[1], part[2], part[3], part[4], part[5], split, True
        ),
        (first_two, second_two, keys_two, values_two, lse_two, context_grad),
    )
    first_low = from_groups(first_grad, row_count).astype(jnp.bfloat16)
    second_low = from_groups(second_grad, row_count).astype(jnp.bfloat16)
    keys_low = from_groups(keys_grad, row_count).astype(jnp.bfloat16)
    values_low = from_groups(values_grad, row_count).astype(jnp.bfloat16)
    grad_ww = weight_grad(word_low, first_low[:, :split])
    grad_ew = weight_grad(entity_low, first_low[:, split:])
    grad_we = weight_grad(word_low, second_low[:, :split])
    grad_ee = weight_grad(entity_low, second_low[:, split:])
    grad_key = weight_grad(low_two, keys_low)
    grad_value = weight_grad(low_two, values_low)
    query_back = jnp.concatenate(
        [
            matmul_back(first_low[:, :split], full_ww)
            + matmul_back(second_low[:, :split], full_we),
            matmul_back(first_low[:, split:], full_ew)
            + matmul_back(second_low[:, split:], full_ee),
        ],
        axis=1,
    )
    tokens_grad = (
        resid_grad
        + matmul_back(keys_low, full_key)
        + matmul_back(values_low, full_value)
        + query_back
    )
    entity_tokens_grad = tokens_grad[:, split:]
    words_grad = tokens_grad[:, :split].astype(jnp.bfloat16)
    entities_grad = entity_tokens_grad.astype(jnp.bfloat16)
    position_grad = jnp.sum(spread_rows(entity_tokens_grad, positions_second, split), axis=0)
    shards = (
        lax.psum_scatter(
            grad_ww.astype(jnp.bfloat16), "narrow", scatter_dimension=0, tiled=True
        ).astype(jnp.float32),
        lax.psum_scatter(
            grad_we.astype(jnp.bfloat16), "narrow", scatter_dimension=0, tiled=True
        ).astype(jnp.float32),
        lax.psum_scatter(
            grad_ew.astype(jnp.bfloat16), "narrow", scatter_dimension=0, tiled=True
        ).astype(jnp.float32),
        lax.psum_scatter(
            grad_ee.astype(jnp.bfloat16), "narrow", scatter_dimension=0, tiled=True
        ).astype(jnp.float32),
        lax.psum_scatter(
            grad_key.astype(jnp.bfloat16), "narrow", scatter_dimension=0, tiled=True
        ).astype(jnp.float32),
        lax.psum_scatter(
            grad_value.astype(jnp.bfloat16), "narrow", scatter_dimension=0, tiled=True
        ).astype(jnp.float32),
        lax.psum_scatter(
            output_grad.astype(jnp.bfloat16), "narrow", scatter_dimension=0, tiled=True
        ).astype(jnp.float32),
        lax.psum_scatter(
            gain_one_grad.astype(jnp.bfloat16), "narrow", scatter_dimension=0, tiled=True
        ).astype(jnp.float32),
        lax.psum_scatter(
            bias_one_grad.astype(jnp.bfloat16), "narrow", scatter_dimension=0, tiled=True
        ).astype(jnp.float32),
        lax.psum_scatter(
            up_grad.astype(jnp.bfloat16), "narrow", scatter_dimension=0, tiled=True
        ).astype(jnp.float32),
        lax.psum_scatter(
            down_grad.astype(jnp.bfloat16), "narrow", scatter_dimension=0, tiled=True
        ).astype(jnp.float32),
        lax.psum_scatter(
            gain_two_grad.astype(jnp.bfloat16), "narrow", scatter_dimension=0, tiled=True
        ).astype(jnp.float32),
        lax.psum_scatter(
            bias_two_grad.astype(jnp.bfloat16), "narrow", scatter_dimension=0, tiled=True
        ).astype(jnp.float32),
        lax.psum_scatter(
            dense_grad.astype(jnp.bfloat16), "narrow", scatter_dimension=0, tiled=True
        ).astype(jnp.float32),
        lax.psum_scatter(
            ew_first.astype(jnp.bfloat16), "narrow", scatter_dimension=0, tiled=True
        ).astype(jnp.float32),
        lax.psum_scatter(
            ee_first.astype(jnp.bfloat16), "narrow", scatter_dimension=0, tiled=True
        ).astype(jnp.float32),
        lax.psum_scatter(
            position_grad.astype(jnp.bfloat16), "narrow", scatter_dimension=0, tiled=True
        ).astype(jnp.float32),
    )
    summed = (
        lax.psum(shards[0].astype(jnp.bfloat16), "wide").astype(jnp.float32),
        lax.psum(shards[1].astype(jnp.bfloat16), "wide").astype(jnp.float32),
        lax.psum(shards[2].astype(jnp.bfloat16), "wide").astype(jnp.float32),
        lax.psum(shards[3].astype(jnp.bfloat16), "wide").astype(jnp.float32),
        lax.psum(shards[4].astype(jnp.bfloat16), "wide").astype(jnp.float32),
        lax.psum(shards[5].astype(jnp.bfloat16), "wide").astype(jnp.float32),
        lax.psum(shards[6].astype(jnp.bfloat16), "wide").astype(jnp.float32),
        lax.psum(shards[7].astype(jnp.bfloat16), "wide").astype(jnp.float32),
        lax.psum(shards[8].astype(jnp.bfloat16), "wide").astype(jnp.float32),
        lax.psum(shards[9].astype(jnp.bfloat16), "wide").astype(jnp.float32),
        lax.psum(shards[10].astype(jnp.bfloat16), "wide").astype(jnp.float32),
        lax.psum(shards[11].astype(jnp.bfloat16), "wide").astype(jnp.float32),
        lax.psum(shards[12].astype(jnp.bfloat16), "wide").astype(jnp.float32),
        lax.psum(shards[13].astype(jnp.bfloat16), "wide").astype(jnp.float32),
        lax.psum(shards[14].astype(jnp.bfloat16), "wide").astype(jnp.float32),
        lax.psum(shards[15].astype(jnp.bfloat16), "wide").astype(jnp.float32),
        lax.psum(shards[16].astype(jnp.bfloat16), "wide").astype(jnp.float32),
    )
    return (
        summed[14],
        summed[15],
        loss_second,
        words_grad,
        entities_grad,
        summed[0],
        summed[1],
        summed[2],
        summed[3],
        summed[4],
        summed[5],
        summed[6],
        summed[7],
        summed[8],
        summed[9],
        summed[10],
        summed[11],
        summed[12],
        table_grad,
        summed[13],
        etable_grad,
        summed[16],
    )


def solution(mesh):
    placed = (
        P(("wide", "narrow"), None, None),
        P(("wide", "narrow"), None, None),
        P(("wide", "narrow"), None),
        P(("wide", "narrow"), None),
        P(("wide", "narrow"), None),
        P(("wide", "narrow"), None, None),
        P(("wide", "narrow"), None, None),
        P(("wide", "narrow"), None),
        P(("wide", "narrow"), None),
        P(("wide", "narrow"), None),
        P(("wide", "narrow"), None),
        P(("wide", "narrow"), None),
        P("narrow", None),
        P("narrow", None),
        P("narrow", None),
        P("narrow", None),
        P("narrow", None),
        P("narrow", None),
        P("narrow", None),
        P("narrow"),
        P("narrow"),
        P("narrow", None),
        P("narrow", None),
        P("narrow"),
        P("narrow"),
        P(("wide", "narrow"), None),
        P("narrow", None),
        P(("wide", "narrow"), None),
        P("narrow", None),
    )
    return jax.shard_map(
        body,
        mesh=mesh,
        in_specs=placed,
        out_specs=(
            P("narrow", None),
            P("narrow", None),
            P(),
            P(("wide", "narrow"), None, None),
            P(("wide", "narrow"), None, None),
            P("narrow", None),
            P("narrow", None),
            P("narrow", None),
            P("narrow", None),
            P("narrow", None),
            P("narrow", None),
            P("narrow", None),
            P("narrow"),
            P("narrow"),
            P("narrow", None),
            P("narrow", None),
            P("narrow"),
            P("narrow"),
            P(("wide", "narrow"), None),
            P("narrow", None),
            P(("wide", "narrow"), None),
            P("narrow", None),
        ),
        check_vma=False,
    )
```

profile of v0, /device:TPU:0, one launch (start us, length us, event | category | flops | bytes accessed | tf_op | source)
XLA Modules:
  0.0 1642.1 jit_solution(917650054354329032)
XLA Ops:
  19.7 8.9 all-reduce.19
  30.4 6.6 all_gather.123
  37.0 12.8 all_gather.111
  53.6 41.2 %all-reduce.15 = (s32[384]{0:T(512)}, s32[2048]{0:T(1024)}, s32[384]{0:T(512)}) all-reduce(s32[384]{0:T(512)S(1)} %fusion.274, s32[2048]{0:T(1024)S(1)} %fusion.272, s32[384]{0:T(512)S(1)} %fusion.276), channel_id=11, replica_groups=mesh['wide'=8,'narrow'=4] {'wide','narrow'}, use_global_device_ids=true, to_apply=%add.5 | all-reduce | flops 2816 | bytes 22528 | tf_op jit(solution)/shard_map/all_gather | solution.py:404
  118.0 11.1 all-gather.45.cloned.1.call-done
  143.0 19.3 %while.77 = (s32[]{:T(128)}, bf16[2,640,6,64]{1,3,2,0:T(8,128)(2,1)}, f32[2,6,640]{2,1,0:T(8,128)S(1)}, bf16[2,640,6,64]{1,3,2,0:T(8,128)(2,1)}, bf16[2,640,6,64...) while((s32[]{:T(128)}, ...), condition=%wide.region_11.12_spmd, body=%wide.region_8.11_spmd.sunk | while | flops 658878720 | bytes 57660140 | solution.py:373
  162.3 3.3 fusion.297
  167.2 19.9 %all-gather.41.cloned.1.call-done = bf16[768,3072]{1,0:T(8,128)(2,1)} async-done(((bf16[192,3072]{1,0:T(8,128)(2,1)}), bf16[768,3072]{1,0:T(8,128)(2,1)}) %all-gather.41.cloned.1.call-update) | async-done | bytes 4718608 | tf_op jit(solution)/shard_map/all_gather | solution.py:320
  187.2 9.4 multiply_convert_fusion.2
  196.6 29.6 %all-gather.43.cloned.1.call-done = bf16[3072,768]{1,0:T(8,128)(2,1)} async-done(((bf16[768,768]{1,0:T(8,128)(2,1)}), bf16[3072,768]{1,0:T(8,128)(2,1)}) %all-gather.43.cloned.1.call-update) | async-done | bytes 4718608 | tf_op jit(solution)/shard_map/all_gather | solution.py:321
  226.2 7.5 fusion.298
  236.8 3.7 gather_fusion.3
  240.6 6.6 while.76
  249.3 3.3 fusion.227
  255.9 40.6 %all-gather.13 = bf16[32,12,256]{2,1,0:T(8,128)(2,1)S(1)} all-gather(bf16[1,12,256]{2,1,0:T(8,128)(2,1)S(1)} %fusion.192), channel_id=1, replica_groups=mesh['wide'=8,'narrow'=4] {'wide','narrow'}, dimensions={0}, use_global_device_ids=true | all-gather | bytes 202752 | tf_op jit(solution)/shard_map/all_gather | solution.py:401
  298.6 36.8 %all-gather.15 = f32[32,1,384]{2,1,0:T(1,128)S(1)} all-gather(f32[1,1,384]{2,1,0:T(1,128)S(1)} %reshape.1246), channel_id=8, replica_groups=mesh['wide'=8,'narrow'=4] {'wide','narrow'}, dimensions={0}, use_global_device_ids=true | all-gather | bytes 50688 | tf_op jit(solution)/shard_map/all_gather | solution.py:16
  336.1 38.2 %all-gather.14 = f32[32,1,384]{2,1,0:T(1,128)S(1)} all-gather(f32[1,1,384]{2,1,0:T(1,128)S(1)} %reshape.1244), channel_id=7, replica_groups=mesh['wide'=8,'narrow'=4] {'wide','narrow'}, dimensions={0}, use_global_device_ids=true | all-gather | bytes 50688 | tf_op jit(solution)/shard_map/all_gather | solution.py:16
  375.7 37.4 %all-gather.16 = bf16[32,12,256]{2,1,0:T(8,128)(2,1)S(1)} all-gather(bf16[1,12,256]{2,1,0:T(8,128)(2,1)S(1)} %fusion.193), channel_id=1, replica_groups=mesh['wide'=8,'narrow'=4] {'wide','narrow'}, dimensions={0}, use_global_device_ids=true | all-gather | bytes 202752 | tf_op jit(solution)/shard_map/all_gather | solution.py:403
  415.4 38.1 %all-gather.18 = f32[32,1,384]{2,1,0:T(1,128)S(1)} all-gather(f32[1,1,384]{2,1,0:T(1,128)S(1)} %reshape.1252), channel_id=10, replica_groups=mesh['wide'=8,'narrow'=4] {'wide','narrow'}, dimensions={0}, use_global_device_ids=true | all-gather | bytes 50688 | tf_op jit(solution)/shard_map/all_gather | solution.py:16
  454.2 36.7 %all-gather.19 = f32[32,1,384]{2,1,0:T(1,128)S(1)} all-gather(f32[1,1,384]{2,1,0:T(1,128)S(1)} %reshape.1254), channel_id=12, replica_groups=mesh['wide'=8,'narrow'=4] {'wide','narrow'}, dimensions={0}, use_global_device_ids=true | all-gather | bytes 50688 | tf_op jit(solution)/shard_map/all_gather | solution.py:16
  491.5 38.1 %all-gather.17 = f32[32,1,384]{2,1,0:T(1,128)S(1)} all-gather(f32[1,1,384]{2,1,0:T(1,128)S(1)} %reshape.1250), channel_id=9, replica_groups=mesh['wide'=8,'narrow'=4] {'wide','narrow'}, dimensions={0}, use_global_device_ids=true | all-gather | bytes 50688 | tf_op jit(solution)/shard_map/all_gather | solution.py:16
  533.8 37.4 %all-gather.4 = f32[65536]{0:T(1024)S(1)} all-gather(f32[2048]{0:T(1024)S(1)} %get-tuple-element.392), channel_id=6, replica_groups=mesh['wide'=8,'narrow'=4] {'wide','narrow'}, dimensions={0}, use_global_device_ids=true | all-gather | bytes 270336 | tf_op jit(solution)/shard_map/all_gather | solution.py:16
  571.2 38.7 %all-gather.1 = f32[65536]{0:T(1024)S(1)} all-gather(f32[2048]{0:T(1024)S(1)} %get-tuple-element.578), channel_id=3, replica_groups=mesh['wide'=8,'narrow'=4] {'wide','narrow'}, dimensions={0}, use_global_device_ids=true | all-gather | bytes 270336 | tf_op jit(solution)/shard_map/all_gather | solution.py:16
  609.9 37.4 %all-gather.2 = f32[65536]{0:T(1024)S(1)} all-gather(f32[2048]{0:T(1024)S(1)} %get-tuple-element.393), channel_id=4, replica_groups=mesh['wide'=8,'narrow'=4] {'wide','narrow'}, dimensions={0}, use_global_device_ids=true | all-gather | bytes 270336 | tf_op jit(solution)/shard_map/all_gather | solution.py:16
  649.7 142.7 %while.78 = (s32[]{:T(128)}, f32[2048]{0:T(1024)S(1)}, f32[2048]{0:T(1024)S(1)}, f32[2048]{0:T(1024)S(1)}, f32[384]{0:T(512)S(1)}, /*index=5*/f32[384]{0:T(512)S...) while((s32[]{:T(128)}, f32[2048]{0:T(1024)S(1)}, ...), condition=%wide.region_25.26_spmd, body=%wide.region_24.25_spmd.sunk | while | flops 19330 | bytes 161481 | solution.py:19
  794.4 4.7 fusion.287
  805.5 73.1 %fusion.293 = (f32[16,256]{1,0:T(8,128)S(1)}, f32[16,256]{1,0:T(8,128)S(1)}) fusion(f32[384,256]{1,0:T(8,128)S(1)} %fusion.308, f32[384,256]{1,0:T(8,128)S(1)} %fusion.198), kind=kCustom, calls=%all-reduce-scatter.2 | all-reduce-scatter fusion | flops 262145 | bytes 819200
  887.7 8.4 collective-permute-start.14
  901.3 12.5 reduce-scatter.27.cloned.1.call-done
  916.2 3.4 multiply_reduce_fusion.2
  921.1 10.6 fusion.166
  931.8 4.5 multiply_reduce_fusion.3
  942.4 69.6 %while.80 = (s32[]{:T(128)}, bf16[2,640,6,64]{1,3,2,0:T(8,128)(2,1)}, bf16[2,640,6,64]{1,3,2,0:T(8,128)(2,1)}, bf16[2,640,6,64]{1,3,2,0:T(8,128)(2,1)}, bf16[2,6...) while((s32[]{:T(128)}, ...), condition=%wide.region_51.52_spmd, body=%wide.region_49.51_spmd.sunk | while | flops 1922830720 | bytes 151980512 | solution.py:495
  952.5 13.8 multiply_convert_fusion.11
  968.1 3.6 fusion.492
  987.1 13.8 multiply_convert_fusion.11
  1002.8 3.6 fusion.492
  1015.7 3.4 collective-permute-start.1
  1020.4 3.8 collective-permute-start.7
  1024.2 3.4 collective-permute-start.3
  1027.6 3.3 collective-permute-start.4
  1030.8 4.2 collective-permute-start.5
  1047.9 7.0 fusion.292
  1059.0 13.9 while.79
  1060.2 4.1 multiply_convert_fusion.10
  1067.2 4.1 multiply_convert_fusion.10
  1091.1 3.3 convolution_convert_fusion.9
  1094.5 3.4 convolution_convert_fusion.11
  1098.0 3.4 convolution_convert_fusion.10
  1106.8 9.1 convolution_convert_fusion.1
  1117.4 8.0 convolution_convert_fusion.2
  1129.5 22.8 %reduce-scatter.25.cloned.1.call-done = bf16[192,768]{1,0:T(8,128)(2,1)} async-done(((bf16[768,768]{1,0:T(8,128)(2,1)}), bf16[192,768]{1,0:T(8,128)(2,1)}) %reduce-scatter.25.cloned.1.call-update) | async-done | bytes 294928 | tf_op jit(solution)/shard_map/reduce_scatter | solution.py:576
  1152.3 26.2 %reduce-scatter.45.cloned.1.call-done = bf16[128,768]{1,0:T(8,128)(2,1)} async-done(((bf16[512,768]{1,0:T(8,128)(2,1)}), bf16[128,768]{1,0:T(8,128)(2,1)}) %reduce-scatter.45.cloned.1.call-update) | async-done | bytes 196624 | tf_op jit(solution)/shard_map/reduce_scatter | solution.py:579
  1178.5 28.0 %reduce-scatter.37.cloned.1.call-done = bf16[192,768]{1,0:T(8,128)(2,1)} async-done(((bf16[768,768]{1,0:T(8,128)(2,1)}), bf16[192,768]{1,0:T(8,128)(2,1)}) %reduce-scatter.37.cloned.1.call-update) | async-done | bytes 294928 | tf_op jit(solution)/shard_map/reduce_scatter | solution.py:549
  1206.6 28.2 %reduce-scatter.33.cloned.1.call-done = bf16[192,768]{1,0:T(8,128)(2,1)} async-done(((bf16[768,768]{1,0:T(8,128)(2,1)}), bf16[192,768]{1,0:T(8,128)(2,1)}) %reduce-scatter.33.cloned.1.call-update) | async-done | bytes 294928 | tf_op jit(solution)/shard_map/reduce_scatter | solution.py:543
  1234.8 28.1 %reduce-scatter.35.cloned.1.call-done = bf16[192,768]{1,0:T(8,128)(2,1)} async-done(((bf16[768,768]{1,0:T(8,128)(2,1)}), bf16[192,768]{1,0:T(8,128)(2,1)}) %reduce-scatter.35.cloned.1.call-update) | async-done | bytes 294928 | tf_op jit(solution)/shard_map/reduce_scatter | solution.py:546
  1262.9 28.2 %reduce-scatter.29.cloned.1.call-done = bf16[192,768]{1,0:T(8,128)(2,1)} async-done(((bf16[768,768]{1,0:T(8,128)(2,1)}), bf16[192,768]{1,0:T(8,128)(2,1)}) %reduce-scatter.29.cloned.1.call-update) | async-done | bytes 294928 | tf_op jit(solution)/shard_map/reduce_scatter | solution.py:537
  1291.1 28.2 %reduce-scatter.31.cloned.1.call-done = bf16[192,768]{1,0:T(8,128)(2,1)} async-done(((bf16[768,768]{1,0:T(8,128)(2,1)}), bf16[192,768]{1,0:T(8,128)(2,1)}) %reduce-scatter.31.cloned.1.call-update) | async-done | bytes 294928 | tf_op jit(solution)/shard_map/reduce_scatter | solution.py:540
  1319.3 50.6 %reduce-scatter.41.cloned.1.call-done = bf16[768,768]{1,0:T(8,128)(2,1)} async-done(((bf16[3072,768]{1,0:T(8,128)(2,1)}), bf16[768,768]{1,0:T(8,128)(2,1)}) %reduce-scatter.41.cloned.1.call-update) | async-done | bytes 1179664 | tf_op jit(solution)/shard_map/reduce_scatter | solution.py:561
  1369.9 50.4 %reduce-scatter.39.cloned.1.call-done = bf16[192,3072]{1,0:T(8,128)(2,1)} async-done(((bf16[768,3072]{1,0:T(8,128)(2,1)}), bf16[192,3072]{1,0:T(8,128)(2,1)}) %reduce-scatter.39.cloned.1.call-update) | async-done | bytes 1179664 | tf_op jit(solution)/shard_map/reduce_scatter | solution.py:558
  1423.8 3.5 fusion.285
  1429.1 5.8 all-reduce.18
  1435.2 22.9 %all-reduce.16 = (bf16[192]{0:T(256)(128)(2,1)S(1)}, bf16[192]{0:T(256)(128)(2,1)S(1)}, bf16[192]{0:T(256)(128)(2,1)S(1)}, bf16[192]{0:T(256)(128)(2,1)S(1)}) all-reduce(bf16[192]{0:T(256)(128)(2,1)S(1)} %dynamic-slice.7, bf16[192]{0:T(256)(128)(2,1)S(1)} %dynamic-slice.9, ...), channel_id=1, replica_groups=mesh['wide'=8,'narrow'=4] {'wide'}, use_global_device_ids=true, to_apply=%region_68.69 | all-reduce | flops 768 | bytes 3072 | tf_op jit(solution)/shard_map/psum | solution.py:591
  1460.4 158.0 %all-reduce.23.cloned.1.call-done = (bf16[192,768]{0,1:T(8,128)(2,1)}, bf16[192,768]{0,1:T(8,128)(2,1)}, bf16[192,768]{1,0:T(8,128)(2,1)}, bf16[192,768]{1,0:T(8...) async-done(((bf16[192,768]{0,1:T(8,128)(2,1)}, ...) | async-done | bytes 5308432 | tf_op jit(solution)/shard_map/psum | solution.py:584
  (1095 shorter events, 387.1 us)
Async XLA Ops:
  7.2 289.3 %copy-start = (bf16[1024,256]{1,0:T(8,128)(2,1)S(1)}, bf16[1024,256]{1,0:T(8,128)(2,1)}, u32[]{:S(2)}) copy-start(bf16[1024,256]{1,0:T(8,128)(2,1)} %param.66) | copy-start | bytes 1572868
  7.2 87.6 %all-gather.35.cloned.1.call-start = ((), (), s32[]{:S(2)}) async-start(), calls=%async_computation.16 | async-start | bytes 1474560 | tf_op jit(solution)/shard_map/all_gather | solution.py:314
  7.9 89.4 %all-gather.33.cloned.1.call-start = ((), (), s32[]{:S(2)}) async-start(), calls=%async_computation.15 | async-start | bytes 1474560 | tf_op jit(solution)/shard_map/all_gather | solution.py:313
  8.8 90.9 %all-gather.37.cloned.1.call-start = ((), (), s32[]{:S(2)}) async-start(), calls=%async_computation.17 | async-start | bytes 1474560 | tf_op jit(solution)/shard_map/all_gather | solution.py:316
  9.5 93.9 %all-gather.31.cloned.1.call-start = ((), (), s32[]{:S(2)}) async-start(), calls=%async_computation.14 | async-start | bytes 1474560 | tf_op jit(solution)/shard_map/all_gather | solution.py:315
  10.1 104.6 %all-gather.47.cloned.1.call-start = ((), (), s32[]{:S(2)}) async-start(), calls=%async_computation.22 | async-start | bytes 1474560 | tf_op jit(solution)/shard_map/all_gather | solution.py:312
  10.7 118.4 %all-gather.45.cloned.1.call-start = ((), (), s32[]{:S(2)}) async-start(), calls=%async_computation.21 | async-start | bytes 1474560 | tf_op jit(solution)/shard_map/all_gather | solution.py:311
  11.3 151.0 %all-gather.39.cloned.1.call-start = ((), (), s32[]{:S(2)}) async-start(), calls=%async_computation.18 | async-start | bytes 1474560 | tf_op jit(solution)/shard_map/all_gather | solution.py:317
  12.0 175.1 %all-gather.41.cloned.1.call-start = ((), (), s32[]{:S(2)}) async-start(), calls=%async_computation.19 | async-start | bytes 5898240 | tf_op jit(solution)/shard_map/all_gather | solution.py:320
  12.8 213.4 %all-gather.43.cloned.1.call-start = ((), (), s32[]{:S(2)}) async-start(), calls=%async_computation.20 | async-start | bytes 5898240 | tf_op jit(solution)/shard_map/all_gather | solution.py:321
  13.5 516.9 %all-gather.49.cloned.1.call-start = ((), (), s32[]{:S(2)}) async-start(), calls=%async_computation.35 | async-start | bytes 3244032 | tf_op jit(solution)/shard_map/all_gather | solution.py:399
  28.6 224.1 %copy-start.127 = (f32[768]{0:T(1024)}, f32[768]{0:T(1024)S(1)}, u32[]{:S(2)}) copy-start(f32[768]{0:T(1024)S(1)} %convert_element_type.526) | copy-start | bytes 9220
  52.1 51.4 %copy-start.47 = (bf16[128,768]{1,0:T(8,128)(2,1)}, bf16[128,768]{1,0:T(8,128)(2,1)S(1)}, u32[]{:S(2)}) copy-start(bf16[128,768]{1,0:T(8,128)(2,1)S(1)} %fusion.229) | copy-start | bytes 589828
  52.2 44.3 %copy-start.62 = (f32[128,768]{1,0:T(8,128)}, f32[128,768]{1,0:T(8,128)S(1)}, u32[]{:S(2)}) copy-start(f32[128,768]{1,0:T(8,128)S(1)} %get-tuple-element.549) | copy-start | bytes 1179652
  52.2 61.4 %copy-start.49 = (bf16[1,128,768]{2,1,0:T(8,128)(2,1)}, bf16[1,128,768]{2,1,0:T(8,128)(2,1)S(1)}, u32[]{:S(2)}) copy-start(bf16[1,128,768]{2,1,0:T(8,128)(2,1)S(1)} %get-tuple-element.548) | copy-start | bytes 589828
  165.6 770.7 %copy-start.121 = (f32[640]{0:T(1024)}, f32[640]{0:T(1024)S(1)}, u32[]{:S(2)}) copy-start(f32[640]{0:T(1024)S(1)} %broadcast_multiply_fusion.5) | copy-start | bytes 7684
  167.2 769.1 %copy-start.130 = (f32[640]{0:T(1024)}, f32[640]{0:T(1024)S(1)}, u32[]{:S(2)}) copy-start(f32[640]{0:T(1024)S(1)} %add_rsqrt_fusion.1) | copy-start | bytes 7684
  233.7 698.0 %copy-start.118 = (f32[640]{0:T(1024)}, f32[640]{0:T(1024)S(1)}, u32[]{:S(2)}) copy-start(f32[640]{0:T(1024)S(1)} %broadcast_multiply_fusion.4) | copy-start | bytes 7684
  234.5 697.3 %copy-start.123 = (f32[640]{0:T(1024)}, f32[640]{0:T(1024)S(1)}, u32[]{:S(2)}) copy-start(f32[640]{0:T(1024)S(1)} %add_rsqrt_fusion) | copy-start | bytes 7684
  240.5 673.2 %reduce-scatter.27.cloned.1.call-start = ((), (), s32[]{:S(2)}) async-start(), calls=%async_computation.25 | async-start | bytes 6488064 | tf_op jit(solution)/shard_map/reduce_scatter | solution.py:440
  254.3 42.7 %copy-start.39 = (f32[1,128,768]{2,1,0:T(8,128)}, f32[1,128,768]{2,1,0:T(8,128)S(1)}, u32[]{:S(2)}) copy-start(f32[1,128,768]{2,1,0:T(8,128)S(1)} %get-tuple-element.583) | copy-start | bytes 1179652
  254.3 42.7 %copy-start.141 = (f32[128]{0:T(128)}, f32[128]{0:T(128)S(1)}, u32[]{:S(2)}) copy-start(f32[128]{0:T(128)S(1)} %broadcast_multiply_fusion.10) | copy-start | bytes 1540
  296.5 78.4 %slice-start.2 = ((bf16[1,640,768]{2,1,0:T(8,128)(2,1)}), bf16[1,128,768]{2,1,0:T(8,128)(2,1)S(1)}, s32[]{:S(2)}) async-start(bf16[1,640,768]{2,1,0:T(8,128)(2,1)} %copy-done.54), calls=%async_computation.41 | async-start | bytes 393216 | tf_op jit(solution)/shard_map/slice | solution.py:379
  296.5 78.4 %copy-start.114 = (s32[12]{0:T(128)S(1)}, s32[12]{0:T(128)}, u32[]{:S(2)}) copy-start(s32[12]{0:T(128)} %or_bitcast_fusion) | copy-start | bytes 148
  336.1 78.8 %copy-start.125 = (s32[1024]{0:T(1024)S(1)}, s32[1024]{0:T(1024)}, u32[]{:S(2)}) copy-start(s32[1024]{0:T(1024)} %iota_add_fusion) | copy-start | bytes 12292
  336.1 78.8 %copy-start.129 = (s32[384]{0:T(512)S(1)}, s32[384]{0:T(512)}, u32[]{:S(2)}) copy-start(s32[384]{0:T(512)} %get-tuple-element.498) | copy-start | bytes 4612
  375.6 39.8 %copy-start.95 = (bf16[12,768]{1,0:T(8,128)(2,1)}, bf16[12,768]{1,0:T(8,128)(2,1)S(1)}, u32[]{:S(2)}) copy-start(bf16[12,768]{1,0:T(8,128)(2,1)S(1)} %gather_fusion.4) | copy-start | bytes 55300
  413.2 40.3 %copy-start.60 = (bf16[384,256]{1,0:T(8,128)(2,1)}, bf16[384,256]{1,0:T(8,128)(2,1)S(1)}, u32[]{:S(2)}) copy-start(bf16[384,256]{1,0:T(8,128)(2,1)S(1)} %reshape.1249) | copy-start | bytes 589828
  413.2 117.3 %copy-start.76 = (bf16[128,768]{1,0:T(8,128)(2,1)S(1)}, bf16[128,768]{1,0:T(8,128)(2,1)}, u32[]{:S(2)}) copy-start(bf16[128,768]{1,0:T(8,128)(2,1)} %param.64) | copy-start | bytes 589828
  533.5 260.9 %copy-start.9 = (f32[2048,128]{0,1:T(8,128)}, f32[2048,128]{0,1:T(8,128)S(1)}, u32[]{:S(2)}) copy-start(f32[2048,128]{0,1:T(8,128)S(1)} %get-tuple-element.579) | copy-start | bytes 3145732
  799.1 326.6 %reduce-scatter.47.cloned.1.call-start = ((), (), s32[]{:S(2)}) async-start(), calls=%async_computation.36 | async-start | bytes 1474560
  804.8 94.8 %copy-start.26 = (bf16[768,256]{1,0:T(8,128)(2,1)S(1)}, bf16[768,256]{1,0:T(8,128)(2,1)}, u32[]{:S(2)}) copy-start(bf16[768,256]{1,0:T(8,128)(2,1)} %all_gather.123) | copy-start | bytes 1179652
  804.8 95.4 %copy-start.162 = (s32[12]{0:T(128)S(1)}, s32[12]{0:T(128)}, u32[]{:S(2)}) copy-start(s32[12]{0:T(128)} %get-tuple-element.570) | copy-start | bytes 148
  804.8 108.9 %copy-start.163 = (s32[64]{0:T(128)S(1)}, s32[64]{0:T(128)}, u32[]{:S(2)}) copy-start(s32[64]{0:T(128)} %get-tuple-element.568) | copy-start | bytes 772
  878.6 9.1 collective-permute-start.9
  879.9 16.3 collective-permute-start.10
  881.2 3.9 collective-permute-start.15
  882.5 15.8 collective-permute-start.11
  883.8 14.5 collective-permute-start.12
  885.1 13.2 collective-permute-start.13
  887.7 10.6 collective-permute-start.14
  896.2 2.5 collective-permute-start.8
  898.7 33.1 %slice-start = ((s8[4718592]{0:T(1024)(128)(4,1)}), s8[524288]{0:T(1024)(128)(4,1)S(1)}, s32[]{:S(2)}) async-start(s8[4718592]{0:T(1024)(128)(4,1)} %bitcast.609), calls=%async_computation.39 | async-start | bytes 1048576
  1015.6 112.0 %reduce-scatter.49.cloned.1.call-start = ((), (), s32[]{:S(2)}) async-start(), calls=%async_computation.37 | async-start | bytes 1474560
  1015.7 19.3 %collective-permute-start.1 = (bf16[16,256]{1,0:T(8,128)(2,1)S(1)}, bf16[16,256]{1,0:T(8,128)(2,1)S(1)}, u32[]{:S(2)}, u32[]{:S(2)}) collective-permute-start(bf16[16,256]{1,0:T(8,128)(2,1)S(1)} %convert.170), channel_id=1, source_target_pairs={{0,2},{1,3},{2,4},{3,5},{4,6},{5,7},{6,8},{7,9},{8,10},{9,11},{10,... | collective-permute-start | bytes 24584
  1019.1 17.6 %collective-permute-start.2 = (bf16[16,256]{1,0:T(8,128)(2,1)S(1)}, bf16[16,256]{1,0:T(8,128)(2,1)S(1)}, u32[]{:S(2)}, u32[]{:S(2)}) collective-permute-start(bf16[16,256]{1,0:T(8,128)(2,1)S(1)} %convert.170), channel_id=1, source_target_pairs={{0,3},{1,4},{2,5},{3,6},{4,7},{5,8},{6,9},{7,10},{8,11},{9,12},{10... | collective-permute-start | bytes 24584
  1020.4 10.4 collective-permute-start.7
  1024.2 15.1 collective-permute-start.3
  1027.6 11.8 collective-permute-start.4
  1030.8 8.5 collective-permute-start.5
  1035.1 4.3 collective-permute-start.6
  1036.7 3.4 collective-permute-start
  1046.8 82.7 %reduce-scatter.43.cloned.1.call-start = ((), (), s32[]{:S(2)}) async-start(), calls=%async_computation.33 | async-start | bytes 491520 | tf_op jit(solution)/shard_map/reduce_scatter | solution.py:570
  1058.9 70.6 %reduce-scatter.23.cloned.1.call-start = ((), (), s32[]{:S(2)}) async-start(), calls=%async_computation.23 | async-start | bytes 1474560 | tf_op jit(solution)/shard_map/reduce_scatter | solution.py:573
  1075.4 76.9 %reduce-scatter.25.cloned.1.call-start = ((), (), s32[]{:S(2)}) async-start(), calls=%async_computation.24 | async-start | bytes 1474560 | tf_op jit(solution)/shard_map/reduce_scatter | solution.py:576
  1077.1 101.5 %reduce-scatter.45.cloned.1.call-start = ((), (), s32[]{:S(2)}) async-start(), calls=%async_computation.34 | async-start | bytes 983040 | tf_op jit(solution)/shard_map/reduce_scatter | solution.py:579
  1090.8 115.8 %reduce-scatter.37.cloned.1.call-start = ((), (), s32[]{:S(2)}) async-start(), calls=%async_computation.30 | async-start | bytes 1474560 | tf_op jit(solution)/shard_map/reduce_scatter | solution.py:549
  1094.4 140.4 %reduce-scatter.33.cloned.1.call-start = ((), (), s32[]{:S(2)}) async-start(), calls=%async_computation.28 | async-start | bytes 1474560 | tf_op jit(solution)/shard_map/reduce_scatter | solution.py:543
  1097.9 165.0 %reduce-scatter.35.cloned.1.call-start = ((), (), s32[]{:S(2)}) async-start(), calls=%async_computation.29 | async-start | bytes 1474560 | tf_op jit(solution)/shard_map/reduce_scatter | solution.py:546
  1101.4 189.7 %reduce-scatter.29.cloned.1.call-start = ((), (), s32[]{:S(2)}) async-start(), calls=%async_computation.26 | async-start | bytes 1474560 | tf_op jit(solution)/shard_map/reduce_scatter | solution.py:537
  1103.9 215.4 %reduce-scatter.31.cloned.1.call-start = ((), (), s32[]{:S(2)}) async-start(), calls=%async_computation.27 | async-start | bytes 1474560 | tf_op jit(solution)/shard_map/reduce_scatter | solution.py:540
  1106.6 263.2 %reduce-scatter.41.cloned.1.call-start = ((), (), s32[]{:S(2)}) async-start(), calls=%async_computation.32 | async-start | bytes 5898240 | tf_op jit(solution)/shard_map/reduce_scatter | solution.py:561
  1115.9 304.4 %reduce-scatter.39.cloned.1.call-start = ((), (), s32[]{:S(2)}) async-start(), calls=%async_computation.31 | async-start | bytes 5898240 | tf_op jit(solution)/shard_map/reduce_scatter | solution.py:558
  1125.4 493.0 %all-reduce.23.cloned.1.call-start = ((), (), s32[]{:S(2)}) async-start(), calls=%async_computation.38 | async-start | bytes 11010048 | tf_op jit(solution)/shard_map/psum | solution.py:584
  (179 other events, 693.8 us)
Sparse Core Ops, SparseCore 0:
  9.6 20.3 all-gather.34
  31.5 21.0 all-gather.32
  54.2 18.1 all-gather.36
  73.8 17.5 all-gather.30
  92.8 17.4 all-gather.46
  111.7 17.4 all-gather.44
  130.7 17.4 all-gather.38
  149.7 37.4 all-gather.40
  188.7 37.4 all-gather.42
  240.6 58.0 all-gather.48
  799.3 114.4 reduce-scatter.26
  1015.8 24.5 reduce-scatter.46
  1047.0 25.4 reduce-scatter.48
  1075.4 20.7 reduce-scatter.42
  1098.6 25.5 reduce-scatter.22
  1126.7 25.6 reduce-scatter.24
  1155.3 23.2 reduce-scatter.44
  1181.0 25.5 reduce-scatter.36
  1209.1 25.6 reduce-scatter.32
  1237.2 25.6 reduce-scatter.34
  1265.4 25.6 reduce-scatter.28
  1293.6 25.6 reduce-scatter.30
  1321.8 47.9 reduce-scatter.40
  1372.3 47.9 reduce-scatter.38
  1426.7 191.5 all-reduce.22
where the time goes:
time: 1660 us; the launch traced here: 1640 us
  blocking collectives  551 us (33%)
  waiting for transfers between devices  529 us (32%)
  matrix products  221 us (13%)
  local copies, waits for them, and re-layouts  219 us (13%)
  other arithmetic  52.5 us (3%)
  starting transfers between devices  44.8 us (3%)
  between operations  22.8 us (1%)
    all_gather x8, blocking collectives, combined_all(): pieces = jax.tree.map(lambda part: lax.all_gather(part, axis), value)  301 us
    psum x1, waiting for transfers between devices, body(): lax.psum(shards[0].astype(jnp.bfloat16), 'wide').astype(jnp.float32)  158 us
    dynamic_slice x217, local copies, waits for them, and re-layouts, combined_all(): lax.scan(lambda subtotal, piece: (join(subtotal, piece), None), head, tail)  140 us
    unnamed x3, blocking collectives  87.9 us
    reduce_scatter x1, waiting for transfers between devices, body(): lax.psum_scatter(down_grad.astype(jnp.bfloat16), 'narrow', scatter_dimens...  50.6 us
    reduce_scatter x1, waiting for transfers between devices, body(): lax.psum_scatter(up_grad.astype(jnp.bfloat16), 'narrow', scatter_dimensio...  50.4 us
    dot_general x16, matrix products, matmul(): jnp.einsum('rld,de->rle', inputs, weight, preferred_element_type=jnp.floa...  45.8 us
    unnamed x18, starting transfers between devices  43.1 us
  transfers between devices with their start and end apart: 41, of which 16 were waited for; matrix products, arithmetic and copies ran while one was open for 16% of the time, Pallas kernels for 0%

commit v1 on v0

--- a/solution.py
+++ b/solution.py
@@ -11,13 +11,179 @@
 HALF_ROOT = 0.7071067811865476
 NORMAL_PEAK = 0.3989422804014327
 
-
-def combined_all(value, axis, join):
-    pieces = jax.tree.map(lambda part: lax.all_gather(part, axis), value)
-    head = jax.tree.map(lambda part: part[0], pieces)
-    tail = jax.tree.map(lambda part: part[1:], pieces)
-    subtotal, _ = lax.scan(lambda subtotal, piece: (join(subtotal, piece), None), head, tail)
-    return subtotal
+WIDTH = 768
+PAD = 16
+
+
+def bits_of(axis):
+    size = lax.axis_size(axis)
+    masks = []
+    mask = 1
+    while mask < size:
+        masks.append(mask)
+        mask *= 2
+    return masks
+
+
+def exchange(value, axis, mask):
+    size = lax.axis_size(axis)
+    return lax.ppermute(value, axis, [(place, place ^ mask) for place in range(size)])
+
+
+def joined_low(mine, theirs):
+    return (mine.astype(jnp.float32) + theirs.astype(jnp.float32)).astype(jnp.bfloat16)
+
+
+def mesh_stages():
+    wide = [("wide", mask) for mask in reversed(bits_of("wide"))]
+    return wide + [("narrow", mask) for mask in reversed(bits_of("narrow"))]
+
+
+def relative_ids():
+    ids = [0]
+    for axis, mask in mesh_stages():
+        step = mask * (lax.axis_size("narrow") if axis == "wide" else 1)
+        ids = ids + [one ^ step for one in ids]
+    return ids
+
+
+def gather_relative(block):
+    value = block[None]
+    for axis, mask in mesh_stages():
+        value = jnp.concatenate([value, exchange(value, axis, mask)], axis=0)
+    return value
+
+
+def scatter_relative(value):
+    for axis, mask in reversed(mesh_stages()):
+        half = value.shape[0] // 2
+        value = joined_low(value[:half], exchange(value[half:], axis, mask))
+    return value[0]
+
+
+def flipped(value, stage):
+    shaped = value.reshape((-1, 2, 1 << stage) + value.shape[1:])
+    return jnp.concatenate([shaped[:, 1:], shaped[:, :1]], axis=1).reshape(value.shape)
+
+
+def join_norms(norms):
+    for stage, (axis, mask) in enumerate(mesh_stages()):
+        theirs = exchange(flipped(norms, stage), axis, mask)
+        top = jnp.maximum(norms, theirs)
+        norms = top + jnp.log(jnp.exp(norms - top) + jnp.exp(theirs - top))
+    return norms
+
+
+def halves(value, axis, mask):
+    side = (lax.axis_index(axis) // mask) % 2
+    mine = lax.dynamic_index_in_dim(value, side, 1, keepdims=False)
+    theirs = lax.dynamic_index_in_dim(value, 1 - side, 1, keepdims=False)
+    return (mine, theirs)
+
+
+def reduce_chunk(blocks):
+    value = blocks
+    rows = blocks.shape[1]
+    for mask in bits_of("narrow"):
+        mine, theirs = halves(value.reshape(value.shape[0] // 2, 2, rows, WIDTH), "narrow", mask)
+        value = joined_low(mine, exchange(theirs, "narrow", mask))
+    value = value[0]
+    for mask in bits_of("wide"):
+        mine, theirs = halves(value.reshape(1, 2, value.shape[0] // 2, WIDTH), "wide", mask)
+        value = joined_low(mine[0], exchange(theirs[0], "wide", mask))
+    for mask in reversed(bits_of("wide")):
+        side = (lax.axis_index("wide") // mask) % 2
+        theirs = exchange(value, "wide", mask)
+        value = jnp.where(
+            side == 0,
+            jnp.concatenate([value, theirs], axis=0),
+            jnp.concatenate([theirs, value], axis=0),
+        )
+    return value
+
+
+def narrow_blocks(grad):
+    count = lax.axis_size("narrow")
+    grad = grad.astype(jnp.bfloat16)
+    rows, columns = grad.shape
+    if columns <= WIDTH:
+        return grad.reshape(count, rows // count * columns // WIDTH, WIDTH)
+    pieces = [
+        grad[:, start : start + WIDTH].reshape(count, rows // count, WIDTH)
+        for start in range(0, columns, WIDTH)
+    ]
+    return jnp.concatenate(pieces, axis=1)
+
+
+def whole_shard(rows, shape):
+    if shape[1] <= WIDTH:
+        return rows.reshape(shape)
+    pieces = jnp.split(rows, shape[1] // WIDTH, axis=0)
+    return jnp.concatenate(pieces, axis=1)
+
+
+def padded_rows(value, multiple):
+    extra = -value.shape[-2] % multiple
+    pads = [(0, 0)] * (value.ndim - 2) + [(0, extra), (0, 0)]
+    return jnp.pad(value, pads) if extra else value
+
+
+def reduce_grads(grads):
+    count = lax.axis_size("narrow")
+    blocks = [narrow_blocks(grad) for grad in grads]
+    packed = padded_rows(jnp.concatenate(blocks, axis=1), PAD * lax.axis_size("wide"))
+    total = reduce_chunk(packed)
+    shards = []
+    start = 0
+    for grad, block in zip(grads, blocks):
+        stop = start + block.shape[1]
+        shape = (grad.shape[0] // count, grad.shape[1])
+        shards.append(whole_shard(total[start:stop], shape).astype(jnp.float32))
+        start = stop
+    return shards
+
+
+def gather_weights(shards):
+    pieces = []
+    for shard in shards:
+        if shard.ndim == 1:
+            pieces.append(jnp.pad(shard, (0, WIDTH - shard.shape[0]))[None])
+        elif shard.shape[1] <= WIDTH:
+            pieces.append(shard.reshape(-1, WIDTH))
+        else:
+            pieces += jnp.split(shard, shard.shape[1] // WIDTH, axis=1)
+    packed = padded_rows(jnp.concatenate(pieces, axis=0), PAD)
+    full = lax.all_gather(packed, "narrow")
+    count = full.shape[0]
+    whole = []
+    start = 0
+    for shard in shards:
+        if shard.ndim == 1:
+            whole.append(full[:, start, : shard.shape[0]].reshape(-1))
+            start += 1
+        elif shard.shape[1] <= WIDTH:
+            rows = shard.shape[0] * shard.shape[1] // WIDTH
+            whole.append(full[:, start : start + rows].reshape(-1, shard.shape[1]))
+            start += rows
+        else:
+            rows = shard.shape[0]
+            blocks = []
+            for _ in range(shard.shape[1] // WIDTH):
+                blocks.append(full[:, start : start + rows].reshape(count * rows, WIDTH))
+                start += rows
+            whole.append(jnp.concatenate(blocks, axis=1))
+    return whole
+
+
+def as_digits(tags):
+    raised = tags + 1
+    digits = jnp.stack([raised % 256, raised // 256 % 256, raised // 65536])
+    return digits.astype(jnp.bfloat16)
+
+
+def from_digits(digits):
+    whole = digits.astype(jnp.int32)
+    return whole[..., 0, :] + 256 * whole[..., 1, :] + 65536 * whole[..., 2, :] - 1
 
 
 def matmul(inputs, weight):
@@ -217,38 +383,22 @@
     )
 
 
-def vocab_stats(rows, tags, table, ids):
+def vocab_part(rows, tags, table, ids):
     logits = jnp.einsum("gd,vd->gv", rows, table, preferred_element_type=jnp.float32)
-    hits = tags[:, None] == ids[None, :]
-    row_top = jnp.max(logits, axis=-1)
-    row_total = jnp.sum(jnp.exp(logits - row_top[:, None]), axis=-1)
-    row_label = jnp.sum(jnp.where(hits, logits, 0.0), axis=-1)
-    return (logits, hits, (row_top, row_total, row_label))
-
-
-def join_stats(first_part, second_part):
-    larger = jnp.maximum(first_part[0], second_part[0])
-    joined = first_part[1] * jnp.exp(first_part[0] - larger) + second_part[1] * jnp.exp(
-        second_part[0] - larger
-    )
-    return (larger, joined, first_part[2] + second_part[2])
-
-
-def join_three(first_part, second_part):
-    return (
-        join_stats(first_part[0:3], second_part[0:3])
-        + join_stats(first_part[3:6], second_part[3:6])
-        + join_stats(first_part[6:9], second_part[6:9])
-    )
-
-
-def vocab_grad(logits, hits, merged, tags, scale):
-    norm = merged[0] + jnp.log(merged[1])
-    valid = (tags >= 0).astype(jnp.float32)
-    logit_grad = (
-        (jnp.exp(logits - norm[:, None]) - hits.astype(jnp.float32)) * (valid * scale)[:, None]
-    ).astype(jnp.bfloat16)
-    return (logit_grad, (norm - merged[2]) * valid)
+    top = jnp.max(logits, axis=-1)
+    total = jnp.sum(jnp.exp(logits - top[:, None]), axis=-1)
+    label = jnp.sum(jnp.where(tags[:, None] == ids[None, :], logits, 0.0), axis=-1)
+    return (logits, top + jnp.log(total), label)
+
+
+def vocab_grad(logits, tags, ids, norms, scales):
+    hits = (tags[:, None] == ids[None, :]).astype(jnp.float32)
+    return ((jnp.exp(logits - norms[:, None]) - hits) * scales[:, None]).astype(jnp.bfloat16)
+
+
+def norm_rows(vectors):
+    columns = jnp.stack(vectors, axis=1)
+    return jnp.pad(columns, ((0, 0), (0, max(lax.axis_size("narrow") - len(vectors), 0))))
 
 
 def tagged(slots, labels):
@@ -292,37 +442,34 @@
     ent_count = entities_second.shape[1]
     length = split + ent_count
     (
-        full_ww,
-        full_we,
+        full_position,
         full_ew,
         full_ee,
         full_key,
         full_value,
-        full_output,
+        full_ww,
+        full_we,
         gain_one,
         bias_one,
-        full_up,
-        full_down,
         gain_two,
         bias_two,
-        full_dense,
-        full_position,
-    ) = (
-        lax.all_gather(query_word_word, "narrow", axis=0, tiled=True),
-        lax.all_gather(query_word_entity, "narrow", axis=0, tiled=True),
-        lax.all_gather(query_entity_word, "narrow", axis=0, tiled=True),
-        lax.all_gather(query_entity_entity, "narrow", axis=0, tiled=True),
-        lax.all_gather(key_weight, "narrow", axis=0, tiled=True),
-        lax.all_gather(value_weight, "narrow", axis=0, tiled=True),
-        lax.all_gather(output_weight, "narrow", axis=0, tiled=True),
-        lax.all_gather(attention_gain, "narrow", axis=0, tiled=True),
-        lax.all_gather(attention_bias, "narrow", axis=0, tiled=True),
-        lax.all_gather(up_weight, "narrow", axis=0, tiled=True),
-        lax.all_gather(down_weight, "narrow", axis=0, tiled=True),
-        lax.all_gather(feedforward_gain, "narrow", axis=0, tiled=True),
-        lax.all_gather(feedforward_bias, "narrow", axis=0, tiled=True),
-        lax.all_gather(entity_dense, "narrow", axis=0, tiled=True),
-        lax.all_gather(position_table, "narrow", axis=0, tiled=True),
+    ) = gather_weights(
+        (
+            position_table,
+            query_entity_word,
+            query_entity_entity,
+            key_weight,
+            value_weight,
+            query_word_word,
+            query_word_entity,
+            attention_gain,
+            attention_bias,
+            feedforward_gain,
+            feedforward_bias,
+        )
+    )
+    full_output, full_up, full_down, full_dense = gather_weights(
+        (output_weight, up_weight, down_weight, entity_dense)
     )
     layer = (gain_one, bias_one, full_up, full_down, gain_two, bias_two)
     ent_width = full_dense.shape[1]
@@ -388,77 +535,104 @@
     word_tags = tagged(word_slots_second, word_labels_second)
     tags_one = tagged(entity_slots_first, entity_labels_first)
     tags_two = tagged(entity_slots_second, entity_labels_second)
-    flat_one = mapped_one.reshape(row_count * ent_slots, ent_width)
-    flat_two = mapped_two.reshape(row_count * ent_slots, ent_width)
+    words_held = row_count * slot_count
+    ents_held = 2 * row_count * ent_slots
+    ent_rows = ents_held * ent_width // WIDTH
+    held = jnp.concatenate([mapped_one.reshape(-1, ent_width), mapped_two.reshape(-1, ent_width)])
+    digits = as_digits(jnp.concatenate([word_tags, tags_one, tags_two])).reshape(-1)
+    tag_rows = -(-digits.shape[0] // WIDTH)
+    digits = jnp.pad(digits, (0, tag_rows * WIDTH - digits.shape[0])).reshape(tag_rows, WIDTH)
+    sent = padded_rows(
+        jnp.concatenate([word_rows, held.reshape(ent_rows, WIDTH), digits]), PAD
+    )
+    gathered = gather_relative(sent)
+    devices = gathered.shape[0]
+    row_stop = words_held + ent_rows
+    all_words = gathered[:, :words_held].reshape(devices * words_held, width)
+    all_held = gathered[:, words_held:row_stop].reshape(devices * ents_held, ent_width)
+    all_digits = gathered[:, row_stop : row_stop + tag_rows].reshape(devices, tag_rows * WIDTH)
+    tag_count = words_held + ents_held
+    all_tags = from_digits(all_digits[:, : 3 * tag_count].reshape(devices, 3, tag_count))
+    valid = (all_tags >= 0).astype(jnp.float32)
+    half_held = words_held + ents_held // 2
+    word_scale = 1.0 / jnp.sum(valid[:, :words_held])
+    scale_one = 1.0 / jnp.sum(valid[:, words_held:half_held])
+    scale_two = 1.0 / jnp.sum(valid[:, half_held:])
+    column = jnp.arange(tag_count)[None, :]
+    scales = valid * jnp.where(
+        column < words_held, word_scale, jnp.where(column < half_held, scale_one, scale_two)
+    )
+    loss_scales = valid * jnp.where(
+        column < words_held, word_scale, jnp.where(column < half_held, 0.0, scale_two)
+    )
+    me = lax.axis_index(("wide", "narrow"))
     word_shard = word_table.shape[0]
     ent_shard = entity_table.shape[0]
-    entity_ids = lax.axis_index(("wide", "narrow")) * ent_shard + jnp.arange(
-        ent_shard, dtype=jnp.int32
-    )
-    all_words, all_word_tags, all_one, all_tags_one, all_two, all_tags_two = (
-        lax.all_gather(word_rows, ("wide", "narrow"), axis=0, tiled=True),
-        lax.all_gather(word_tags, ("wide", "narrow"), axis=0, tiled=True),
-        lax.all_gather(flat_one, ("wide", "narrow"), axis=0, tiled=True),
-        lax.all_gather(tags_one, ("wide", "narrow"), axis=0, tiled=True),
-        lax.all_gather(flat_two, ("wide", "narrow"), axis=0, tiled=True),
-        lax.all_gather(tags_two, ("wide", "narrow"), axis=0, tiled=True),
-    )
-    word_scale = 1.0 / jnp.sum(all_word_tags >= 0).astype(jnp.float32)
-    scale_one = 1.0 / jnp.sum(all_tags_one >= 0).astype(jnp.float32)
-    scale_two = 1.0 / jnp.sum(all_tags_two >= 0).astype(jnp.float32)
-    word_ids = lax.axis_index(("wide", "narrow")) * word_shard + jnp.arange(
-        word_shard, dtype=jnp.int32
-    )
-    word_logits, word_hits, word_stats = vocab_stats(all_words, all_word_tags, word_table, word_ids)
-    logits_one, hits_one, stats_one = vocab_stats(all_one, all_tags_one, entity_table, entity_ids)
-    logits_two, hits_two, stats_two = vocab_stats(all_two, all_tags_two, entity_table, entity_ids)
-    merged = combined_all(
-        (
-            word_stats[0],
-            word_stats[1],
-            word_stats[2],
-            stats_one[0],
-            stats_one[1],
-            stats_one[2],
-            stats_two[0],
-            stats_two[1],
-            stats_two[2],
-        ),
-        ("wide", "narrow"),
-        join_three,
-    )
-    word_grad_low, word_terms = vocab_grad(
-        word_logits, word_hits, merged[0:3], all_word_tags, word_scale
-    )
-    grad_one_low, terms_one = vocab_grad(logits_one, hits_one, merged[3:6], all_tags_one, scale_one)
-    grad_two_low, terms_two = vocab_grad(logits_two, hits_two, merged[6:9], all_tags_two, scale_two)
+    word_ids = me * word_shard + jnp.arange(word_shard, dtype=jnp.int32)
+    entity_ids = me * ent_shard + jnp.arange(ent_shard, dtype=jnp.int32)
+    flat_word_tags = all_tags[:, :words_held].reshape(-1)
+    flat_ent_tags = all_tags[:, words_held:].reshape(-1)
+    word_logits, word_norms, word_label = vocab_part(
+        all_words, flat_word_tags, word_table, word_ids
+    )
+    ent_logits, ent_norms, ent_label = vocab_part(
+        all_held, flat_ent_tags, entity_table, entity_ids
+    )
+    norms = join_norms(
+        jnp.concatenate(
+            [word_norms.reshape(devices, words_held), ent_norms.reshape(devices, ents_held)], axis=1
+        )
+    )
+    word_grad_low = vocab_grad(
+        word_logits,
+        flat_word_tags,
+        word_ids,
+        norms[:, :words_held].reshape(-1),
+        scales[:, :words_held].reshape(-1),
+    )
+    ent_grad_low = vocab_grad(
+        ent_logits,
+        flat_ent_tags,
+        entity_ids,
+        norms[:, words_held:].reshape(-1),
+        scales[:, words_held:].reshape(-1),
+    )
+    labels = jnp.concatenate(
+        [word_label.reshape(devices, words_held), ent_label.reshape(devices, ents_held)], axis=1
+    )
+    loss_part = jnp.sum(norms[0] * loss_scales[0]) - jnp.sum(labels * loss_scales)
+    partial_rows = jnp.einsum(
+        "gv,vd->gd", word_grad_low, word_table, preferred_element_type=jnp.float32
+    ).astype(jnp.bfloat16)
+    partial_held = jnp.einsum(
+        "gv,ve->ge", ent_grad_low, entity_table, preferred_element_type=jnp.float32
+    ).astype(jnp.bfloat16)
+    returned = scatter_relative(
+        jnp.concatenate(
+            [
+                partial_rows.reshape(devices, words_held, WIDTH),
+                partial_held.reshape(devices, ent_rows, WIDTH),
+            ],
+            axis=1,
+        )
+    )
+    word_rows_grad = returned[:words_held].astype(jnp.float32)
+    map_low = returned[words_held:].reshape(2, row_count, ent_slots, ent_width)
+    map_low_one, map_low_two = map_low[0], map_low[1]
     table_grad = jnp.einsum(
         "gv,gd->vd", word_grad_low, all_words, preferred_element_type=jnp.float32
     )
-    etable_grad = jnp.einsum("gv,ge->ve", grad_two_low, all_two, preferred_element_type=jnp.float32)
-    word_rows_grad, map_grad_one, map_grad_two = (
-        lax.psum_scatter(
-            jnp.einsum("gv,vd->gd", word_grad_low, word_table, preferred_element_type=jnp.float32),
-            ("wide", "narrow"),
-            scatter_dimension=0,
-            tiled=True,
-        ),
-        lax.psum_scatter(
-            jnp.einsum("gv,ve->ge", grad_one_low, entity_table, preferred_element_type=jnp.float32),
-            ("wide", "narrow"),
-            scatter_dimension=0,
-            tiled=True,
-        ),
-        lax.psum_scatter(
-            jnp.einsum("gv,ve->ge", grad_two_low, entity_table, preferred_element_type=jnp.float32),
-            ("wide", "narrow"),
-            scatter_dimension=0,
-            tiled=True,
-        ),
-    )
-    loss_second = jnp.sum(word_terms) * word_scale + jnp.sum(terms_two) * scale_two
-    map_low_one = map_grad_one.astype(jnp.bfloat16).reshape(row_count, ent_slots, ent_width)
-    map_low_two = map_grad_two.astype(jnp.bfloat16).reshape(row_count, ent_slots, ent_width)
+    second_held = jnp.where(
+        jnp.arange(ents_held)[None, :, None] >= ents_held // 2,
+        all_held.reshape(devices, ents_held, ent_width),
+        jnp.zeros((), jnp.bfloat16),
+    ).reshape(-1, ent_width)
+    etable_grad = jnp.einsum(
+        "gv,ge->ve", ent_grad_low, second_held, preferred_element_type=jnp.float32
+    )
+    loss_second = loss_part
+    for axis, mask in mesh_stages():
+        loss_second = loss_second + exchange(loss_second, axis, mask)
     entity_grad_one = entity_back(
         map_low_one, picked_one, entity_slots_first, full_dense, ent_count, False
     )[0]
@@ -527,101 +701,43 @@
     words_grad = tokens_grad[:, :split].astype(jnp.bfloat16)
     entities_grad = entity_tokens_grad.astype(jnp.bfloat16)
     position_grad = jnp.sum(spread_rows(entity_tokens_grad, positions_second, split), axis=0)
-    shards = (
-        lax.psum_scatter(
-            grad_ww.astype(jnp.bfloat16), "narrow", scatter_dimension=0, tiled=True
-        ).astype(jnp.float32),
-        lax.psum_scatter(
-            grad_we.astype(jnp.bfloat16), "narrow", scatter_dimension=0, tiled=True
-        ).astype(jnp.float32),
-        lax.psum_scatter(
-            grad_ew.astype(jnp.bfloat16), "narrow", scatter_dimension=0, tiled=True
-        ).astype(jnp.float32),
-        lax.psum_scatter(
-            grad_ee.astype(jnp.bfloat16), "narrow", scatter_dimension=0, tiled=True
-        ).astype(jnp.float32),
-        lax.psum_scatter(
-            grad_key.astype(jnp.bfloat16), "narrow", scatter_dimension=0, tiled=True
-        ).astype(jnp.float32),
-        lax.psum_scatter(
-            grad_value.astype(jnp.bfloat16), "narrow", scatter_dimension=0, tiled=True
-        ).astype(jnp.float32),
-        lax.psum_scatter(
-            output_grad.astype(jnp.bfloat16), "narrow", scatter_dimension=0, tiled=True
-        ).astype(jnp.float32),
-        lax.psum_scatter(
-            gain_one_grad.astype(jnp.bfloat16), "narrow", scatter_dimension=0, tiled=True
-        ).astype(jnp.float32),
-        lax.psum_scatter(
-            bias_one_grad.astype(jnp.bfloat16), "narrow", scatter_dimension=0, tiled=True
-        ).astype(jnp.float32),
-        lax.psum_scatter(
-            up_grad.astype(jnp.bfloat16), "narrow", scatter_dimension=0, tiled=True
-        ).astype(jnp.float32),
-        lax.psum_scatter(
-            down_grad.astype(jnp.bfloat16), "narrow", scatter_dimension=0, tiled=True
-        ).astype(jnp.float32),
-        lax.psum_scatter(
-            gain_two_grad.astype(jnp.bfloat16), "narrow", scatter_dimension=0, tiled=True
-        ).astype(jnp.float32),
-        lax.psum_scatter(
-            bias_two_grad.astype(jnp.bfloat16), "narrow", scatter_dimension=0, tiled=True
-        ).astype(jnp.float32),
-        lax.psum_scatter(
-            dense_grad.astype(jnp.bfloat16), "narrow", scatter_dimension=0, tiled=True
-        ).astype(jnp.float32),
-        lax.psum_scatter(
-            ew_first.astype(jnp.bfloat16), "narrow", scatter_dimension=0, tiled=True
-        ).astype(jnp.float32),
-        lax.psum_scatter(
-            ee_first.astype(jnp.bfloat16), "narrow", scatter_dimension=0, tiled=True
-        ).astype(jnp.float32),
-        lax.psum_scatter(
-            position_grad.astype(jnp.bfloat16), "narrow", scatter_dimension=0, tiled=True
-        ).astype(jnp.float32),
-    )
-    summed = (
-        lax.psum(shards[0].astype(jnp.bfloat16), "wide").astype(jnp.float32),
-        lax.psum(shards[1].astype(jnp.bfloat16), "wide").astype(jnp.float32),
-        lax.psum(shards[2].astype(jnp.bfloat16), "wide").astype(jnp.float32),
-        lax.psum(shards[3].astype(jnp.bfloat16), "wide").astype(jnp.float32),
-        lax.psum(shards[4].astype(jnp.bfloat16), "wide").astype(jnp.float32),
-        lax.psum(shards[5].astype(jnp.bfloat16), "wide").astype(jnp.float32),
-        lax.psum(shards[6].astype(jnp.bfloat16), "wide").astype(jnp.float32),
-        lax.psum(shards[7].astype(jnp.bfloat16), "wide").astype(jnp.float32),
-        lax.psum(shards[8].astype(jnp.bfloat16), "wide").astype(jnp.float32),
-        lax.psum(shards[9].astype(jnp.bfloat16), "wide").astype(jnp.float32),
-        lax.psum(shards[10].astype(jnp.bfloat16), "wide").astype(jnp.float32),
-        lax.psum(shards[11].astype(jnp.bfloat16), "wide").astype(jnp.float32),
-        lax.psum(shards[12].astype(jnp.bfloat16), "wide").astype(jnp.float32),
-        lax.psum(shards[13].astype(jnp.bfloat16), "wide").astype(jnp.float32),
-        lax.psum(shards[14].astype(jnp.bfloat16), "wide").astype(jnp.float32),
-        lax.psum(shards[15].astype(jnp.bfloat16), "wide").astype(jnp.float32),
-        lax.psum(shards[16].astype(jnp.bfloat16), "wide").astype(jnp.float32),
+    down_sum, up_sum = reduce_grads((down_grad, up_grad))
+    output_sum, dense_sum, ew_first_sum, ee_first_sum, norm_sum = reduce_grads(
+        (
+            output_grad,
+            dense_grad,
+            ew_first,
+            ee_first,
+            norm_rows((gain_one_grad, bias_one_grad, gain_two_grad, bias_two_grad)),
+        )
+    )
+    ww_sum, we_sum, key_sum = reduce_grads((grad_ww, grad_we, grad_key))
+    ew_sum, ee_sum, value_sum, position_sum = reduce_grads(
+        (grad_ew, grad_ee, grad_value, position_grad)
     )
     return (
-        summed[14],
-        summed[15],
+        ew_first_sum,
+        ee_first_sum,
         loss_second,
         words_grad,
         entities_grad,
-        summed[0],
-        summed[1],
-        summed[2],
-        summed[3],
-        summed[4],
-        summed[5],
-        summed[6],
-        summed[7],
-        summed[8],
-        summed[9],
-        summed[10],
-        summed[11],
-        summed[12],
+        ww_sum,
+        we_sum,
+        ew_sum,
+        ee_sum,
+        key_sum,
+        value_sum,
+        output_sum,
+        norm_sum[:, 0],
+        norm_sum[:, 1],
+        up_sum,
+        down_sum,
+        norm_sum[:, 2],
+        norm_sum[:, 3],
         table_grad,
-        summed[13],
+        dense_sum,
         etable_grad,
-        summed[16],
+        position_sum,
     )
 
 

time: 1660 us -> 890 us (0.54)
  blocking collectives: 551 us -> 0 us
  waiting for transfers between devices: 529 us -> 270 us
  starting transfers between devices: 44.8 us -> 138 us
  local copies, waits for them, and re-layouts: 219 us -> 152 us
  other arithmetic: 52.5 us -> 75.4 us
    all_gather x13 -> x0, blocking collectives: 440 us -> none  [the longest x8 301 us: combined_all(): pieces = jax.tree.map(lambda part: lax.all_gather(part, axis), value)]
    reduce_scatter x12 -> x0, waiting for transfers between devices: 303 us -> none  [the longest x1 50.6 us: body(): lax.psum_scatter(down_grad.astype(jnp.bfloat16), 'narrow', scatter_dimens...]
    ppermute x0 -> x52, waiting for transfers between devices: none -> 226 us  [exchange(): lax.ppermute(value, axis, [(place, place ^ mask) for place in range(size)])]
    psum x1 -> x0, waiting for transfers between devices: 158 us -> none  [body(): lax.psum(shards[0].astype(jnp.bfloat16), 'wide').astype(jnp.float32)]
    dynamic_slice x217 -> x0, local copies, waits for them, and re-layouts: 140 us -> none  [combined_all(): lax.scan(lambda subtotal, piece: (join(subtotal, piece), None), head, tail)]
    ppermute x0 -> x52, starting transfers between devices: none -> 138 us  [exchange(): lax.ppermute(value, axis, [(place, place ^ mask) for place in range(size)])]
    unnamed x3 -> x0, blocking collectives: 87.9 us -> none
    unnamed x18 -> x0, starting transfers between devices: 43.1 us -> none
  transfers between devices with their start and end apart: 41 -> 54, of which waited for: 16 -> 36; matrix products, arithmetic and copies ran while one was open for 16% -> 17% of each run, Pallas kernels for 0% -> 0%
where the time goes in v1:
time: 890 us; the launch traced here: 878 us
  waiting for transfers between devices  270 us (30%)
  matrix products  216 us (24%)
  local copies, waits for them, and re-layouts  152 us (17%)
  starting transfers between devices  138 us (16%)
  other arithmetic  75.4 us (8%)
  between operations  25.3 us (3%)
    ppermute x52, waiting for transfers between devices, exchange(): lax.ppermute(value, axis, [(place, place ^ mask) for place in range(size)])  226 us
    ppermute x52, starting transfers between devices, exchange(): lax.ppermute(value, axis, [(place, place ^ mask) for place in range(size)])  138 us
    all_gather x2, waiting for transfers between devices, gather_weights(): full = lax.all_gather(packed, 'narrow')  44.2 us
    unnamed x360, local copies, waits for them, and re-layouts  42 us
    dot_general x11, matrix products, matmul_back(): jnp.einsum('rle,de->rld', grads, weight, preferred_element_type=jnp.float32)  38.6 us
    dot_general x16, matrix products, matmul(): jnp.einsum('rld,de->rle', inputs, weight, preferred_element_type=jnp.floa...  38.1 us
    dot_general x11, matrix products, weight_grad(): jnp.einsum('rld,rle->de', inputs, grads, preferred_element_type=jnp.float32)  28.6 us
    sub x2, matrix products, attention_backward(): probs_grad - jnp.sum(probs * probs_grad, axis=-1, keepdims=True)  27.5 us
  transfers between devices with their start and end apart: 54, of which 36 were waited for; matrix products, arithmetic and copies ran while one was open for 17% of the time, Pallas kernels for 0%

profile of v1, /device:TPU:0, one launch (start us, length us, event | category | flops | bytes accessed | tf_op | source)
XLA Modules:
  0.0 877.7 jit_solution(5278495867810790283)
XLA Ops:
  10.0 11.8 %concatenate.298 = bf16[1284,768]{1,0:T(8,128)(2,1)S(1)} concatenate(bf16[128,768]{1,0:T(8,128)(2,1)} %param.65, bf16[192,768]{1,0:T(8,128)(2,1)} %param.51, bf16[192,768]{1,0:T(8,128)(2,1)} %param.52, bf16[192,768]{1,0:T(8,128)(2,1)} %param.53, bf16[192,768]{1,0:T(8,128)(2,1)} %param.54, bf16[192,768]{1,0:T(8,128)(2,1)} %param.49, bf16[192,768]{1,0:T(8,128)(2,1)} %param.50, ...), dimensions={0} | concatenate | bytes 3944448 | tf_op jit(solution)/shard_map/concatenate | solution.py:155
  37.8 44.2 %all-gather.5.cloned.1.call-done = bf16[5184,768]{1,0:T(8,128)(2,1)} async-done(((bf16[1296,768]{1,0:T(8,128)(2,1)}), bf16[5184,768]{1,0:T(8,128)(2,1)}) %all-gather.5.cloned.1.call-update) | async-done | bytes 7962640 | tf_op jit(solution)/shard_map/all_gather | solution.py:156
  85.9 5.8 fusion.332
  101.9 3.5 convolution_convert_fusion.16
  116.1 3.5 convolution_convert_fusion.15
  124.3 3.1 convolution_convert_fusion.14
  136.1 6.4 while.53
  143.6 19.3 %while.52 = (s32[]{:T(128)}, bf16[2,640,6,64]{1,3,2,0:T(8,128)(2,1)}, f32[2,6,640]{2,1,0:T(8,128)S(1)}, bf16[2,640,6,64]{1,3,2,0:T(8,128)(2,1)}, bf16[2,640,6,64...) while((s32[]{:T(128)}, ...), condition=%wide.region_3.4_spmd, body=%wide.region_0.3_spmd.sunk | while | flops 658878720 | bytes 57660140 | solution.py:520
  162.9 3.1 fusion.331
  166.1 4.7 slice.472
  174.9 6.5 multiply_convert_fusion.2
  181.4 3.4 fusion.341
  190.9 5.3 fusion.245
  203.4 6.8 collective-permute-done
  210.6 7.0 collective-permute-done.1
  219.1 10.3 %collective-permute-done.2 = bf16[4,80,768]{2,1,0:T(8,128)(2,1)S(1)} collective-permute-done((bf16[4,80,768]{2,1,0:T(8,128)(2,1)S(1)}, bf16[4,80,768]{2,1,0:T(8,128)(2,1)S(1)}, u32[]{:S(2)}, u32[]{:S(2)}) %collective-permute-start.2) | collective-permute-done | bytes 491552 | tf_op jit(solution)/shard_map/ppermute | solution.py:30
  233.4 17.5 %collective-permute-done.3 = bf16[8,80,768]{2,1,0:T(8,128)(2,1)S(1)} collective-permute-done((bf16[8,80,768]{2,1,0:T(8,128)(2,1)S(1)}, bf16[8,80,768]{2,1,0:T(8,128)(2,1)S(1)}, u32[]{:S(2)}, u32[]{:S(2)}) %collective-permute-start.3) | collective-permute-done | bytes 983072 | tf_op jit(solution)/shard_map/ppermute | solution.py:30
  252.4 4.3 collective-permute-done.4
  256.7 3.0 constant_dynamic-update-slice_fusion.8
  261.7 3.9 slice.478
  269.7 3.0 fusion.345
  273.3 4.5 collective-permute-start.5
  301.3 3.3 collective-permute-done.10
  306.1 21.0 %collective-permute-done.11 = bf16[8,72,768]{2,1,0:T(8,128)(2,1)S(1)} collective-permute-done((bf16[8,72,768]{2,1,0:T(8,128)(2,1)S(1)}, bf16[8,72,768]{2,1,0:T(8,128)(2,1)S(1)}, u32[]{:S(2)}, u32[]{:S(2)}) %collective-permute-start.11) | collective-permute-done | bytes 884768 | tf_op jit(solution)/shard_map/ppermute | solution.py:30
  329.0 10.1 %collective-permute-done.12 = bf16[4,72,768]{2,1,0:T(8,128)(2,1)S(1)} collective-permute-done((bf16[4,72,768]{2,1,0:T(8,128)(2,1)S(1)}, bf16[4,72,768]{2,1,0:T(8,128)(2,1)S(1)}, u32[]{:S(2)}, u32[]{:S(2)}) %collective-permute-start.12) | collective-permute-done | bytes 442400 | tf_op jit(solution)/shard_map/ppermute | solution.py:30
  340.3 5.0 collective-permute-done.13
  348.8 3.5 collective-permute-done.14
  360.8 11.4 %fusion.164 = bf16[640,3072]{1,0:T(8,128)(2,1)} fusion(f32[640,3072]{1,0:T(8,128)} %get-tuple-element.377, bf16[3072,768]{1,0:T(8,128)(2,1)S(1)} %bitcast.740, f32[640,768]{1,0:T(8,128)S(1)} %copy-done.20, f32[128,768]{1,0:T(8,128)S(1)} %get-tuple-element.395, f32[512,768]{1,0:T(8,128)S(1)} %get-tuple-element.393, f32[640]{0:T(1024)S(1)} %broadcast_multiply_fusion.2, ...), kind=kOutput, calls=%fused_computation.170 | convolution fusion | flops 3043983360 | bytes 20460544 | tf_op jit(solution)/shard_map/rle,de->rld/dot_general | solution.py:194
  372.2 6.8 multiply_reduce_fusion.3
  386.6 76.3 %while.55 = (s32[]{:T(128)}, bf16[2,640,6,64]{1,3,2,0:T(8,128)(2,1)}, bf16[2,640,6,64]{1,3,2,0:T(8,128)(2,1)}, bf16[2,640,6,64]{1,3,2,0:T(8,128)(2,1)}, bf16[2,6...) while((s32[]{:T(128)}, ...), condition=%wide.region_45.46_spmd, body=%wide.region_43.45_spmd.sunk | while | flops 1922830720 | bytes 124455360 | solution.py:669
  389.5 5.4 fusion.515
  394.9 13.8 %multiply_convert_fusion.9 = bf16[6,640,640]{1,2,0:T(8,128)(2,1)} fusion(f32[6,640]{1,0:T(8,128)S(1)} %dynamic-slice_bitcast_fusion.65, f32[6,640,128]{1,2,0:T(8,128)} %fusion.514, f32[6,640,512]{1,2,0:T(8,128)} %fusion.515, bf16[2,640,6,64]{1,3,2,0:T(8,128)(2,1)} %get-tuple-element.742, s32[]{:T(128)S(6)} %copy.167, ...), kind=kOutput, calls=%fused_computation.96.clone.1 | convolution fusion | flops 653726080 | bytes 26585088 | tf_op jit(solution)/shard_map/while/body/eval_jaxpr/sub | solution.py:272
  408.7 4.0 fusion.516
  416.4 3.6 fusion.518
  427.6 5.4 fusion.515
  432.9 13.7 %multiply_convert_fusion.9 = bf16[6,640,640]{1,2,0:T(8,128)(2,1)} fusion(f32[6,640]{1,0:T(8,128)S(1)} %dynamic-slice_bitcast_fusion.65, f32[6,640,128]{1,2,0:T(8,128)} %fusion.514, f32[6,640,512]{1,2,0:T(8,128)} %fusion.515, bf16[2,640,6,64]{1,3,2,0:T(8,128)(2,1)} %get-tuple-element.742, s32[]{:T(128)S(6)} %copy.167, ...), kind=kOutput, calls=%fused_computation.96.clone.1 | convolution fusion | flops 653726080 | bytes 26585088 | tf_op jit(solution)/shard_map/while/body/eval_jaxpr/sub | solution.py:272
  446.7 4.0 fusion.516
  454.4 3.6 fusion.518
  462.9 4.0 fusion.352
  477.2 7.0 convolution_convert_fusion.2
  484.3 6.3 convolution_convert_fusion.1
  493.6 8.5 fusion.329
  504.6 19.3 %while.54 = (s32[]{:T(128)}, bf16[2,128,6,64]{1,3,2,0:T(8,128)(2,1)}, bf16[2,128,6,64]{1,3,2,0:T(8,128)(2,1)}, bf16[2,640,6,64]{1,3,2,0:T(8,128)(2,1)S(1)}, bf16...) while((s32[]{:T(128)}, ...), condition=%wide.region_33.34_spmd, body=%wide.region_31.33_spmd.sunk | while | flops 193758592 | bytes 15154429 | solution.py:645
  508.7 4.1 multiply_convert_fusion.8
  518.2 4.1 multiply_convert_fusion.8
  569.2 3.1 collective-permute-start.23
  572.3 3.1 fusion.172
  581.9 8.7 collective-permute-done.29
  593.7 3.6 fusion.158
  614.2 75.1 %collective-permute-start.26 = (f32[]{:T(128)}, f32[]{:T(128)}, u32[]{:S(2)}, u32[]{:S(2)}) collective-permute-start(f32[]{:T(128)} %add.665), channel_id=1, source_target_pairs={{0,2},{1,3},{2,0},{3,1},{4,6},{5,7},{6,4},{7,5},{8,10},{9,11},{10,... | collective-permute-start | bytes 20 | tf_op jit(solution)/shard_map/ppermute | solution.py:30
  711.0 4.3 collective-permute-done.32
  719.4 4.2 collective-permute-done.33
  726.1 4.2 collective-permute-done.38
  734.3 4.2 collective-permute-done.18
  738.6 16.9 %collective-permute-done.46 = bf16[768,768]{1,0:T(8,128)(2,1)S(1)} collective-permute-done((bf16[768,768]{1,0:T(8,128)(2,1)S(1)}, bf16[768,768]{1,0:T(8,128)(2,1)S(1)}, u32[]{:S(2)}, u32[]{:S(2)}) %collective-permute-start.46) | collective-permute-done | bytes 1179680 | tf_op jit(solution)/shard_map/ppermute | solution.py:30
  760.5 13.5 %collective-permute-done.19 = bf16[96,768]{1,0:T(8,128)(2,1)S(1)} collective-permute-done((bf16[96,768]{1,0:T(8,128)(2,1)S(1)}, bf16[96,768]{1,0:T(8,128)(2,1)S(1)}, u32[]{:S(2)}, u32[]{:S(2)}) %collective-permute-start.19) | collective-permute-done | bytes 147488 | tf_op jit(solution)/shard_map/ppermute | solution.py:30
  774.1 3.5 collective-permute-start.20
  780.9 13.3 %collective-permute-done.20 = bf16[96,768]{1,0:T(8,128)(2,1)S(1)} collective-permute-done((bf16[96,768]{1,0:T(8,128)(2,1)S(1)}, bf16[96,768]{1,0:T(8,128)(2,1)S(1)}, u32[]{:S(2)}, u32[]{:S(2)}) %collective-permute-start.20) | collective-permute-done | bytes 147488 | tf_op jit(solution)/shard_map/ppermute | solution.py:30
  794.3 6.3 collective-permute-done.48
  801.1 7.2 collective-permute-done.21
  810.4 4.7 collective-permute-done.49
  816.7 4.7 collective-permute-done.42
  824.4 9.7 %collective-permute-done.50 = bf16[384,768]{1,0:T(8,128)(2,1)} collective-permute-done((bf16[384,768]{1,0:T(8,128)(2,1)S(1)}, bf16[384,768]{1,0:T(8,128)(2,1)}, u32[]{:S(2)}, u32[]{:S(2)}) %collective-permute-start.50) | collective-permute-done | bytes 589856 | tf_op jit(solution)/shard_map/ppermute | solution.py:30
  844.0 20.0 %collective-permute-done.51 = bf16[768,768]{1,0:T(8,128)(2,1)} collective-permute-done((bf16[768,768]{1,0:T(8,128)(2,1)S(1)}, bf16[768,768]{1,0:T(8,128)(2,1)}, u32[]{:S(2)}, u32[]{:S(2)}) %collective-permute-start.51) | collective-permute-done | bytes 1179680 | tf_op jit(solution)/shard_map/ppermute | solution.py:30
  (866 shorter events, 337.1 us)
Async XLA Ops:
  7.2 259.1 %copy-start = (bf16[1024,256]{1,0:T(8,128)(2,1)S(1)}, bf16[1024,256]{1,0:T(8,128)(2,1)}, u32[]{:S(2)}) copy-start(bf16[1024,256]{1,0:T(8,128)(2,1)} %param.64) | copy-start | bytes 1572868
  7.2 74.8 %all-gather.5.cloned.1.call-start = ((), (), s32[]{:S(2)}) async-start(), calls=%async_computation | async-start | bytes 9953280 | tf_op jit(solution)/shard_map/all_gather | solution.py:156
  23.3 139.6 %all-gather.7.cloned.1.call-start = ((), (), s32[]{:S(2)}) async-start(), calls=%async_computation.1 | async-start | bytes 13762560 | tf_op jit(solution)/shard_map/all_gather | solution.py:156
  37.8 47.3 %copy-start.45 = (f32[512,768]{1,0:T(8,128)}, f32[512,768]{1,0:T(8,128)S(1)}, u32[]{:S(2)}) copy-start(f32[512,768]{1,0:T(8,128)S(1)} %bitcast_convert_fusion) | copy-start | bytes 4718596
  85.0 49.5 %copy-start.51 = (bf16[1,128,768]{2,1,0:T(8,128)(2,1)}, bf16[1,128,768]{2,1,0:T(8,128)(2,1)S(1)}, u32[]{:S(2)}) copy-start(bf16[1,128,768]{2,1,0:T(8,128)(2,1)S(1)} %get-tuple-element.342) | copy-start | bytes 589828
  91.7 37.3 %copy-start.12 = (bf16[4,192,768]{2,1,0:T(8,128)(2,1)}, bf16[4,192,768]{2,1,0:T(8,128)(2,1)S(1)}, u32[]{:S(2)}) copy-start(bf16[4,192,768]{2,1,0:T(8,128)(2,1)S(1)} %get-tuple-element.316) | copy-start | bytes 3538948
  188.9 164.0 %copy-start.30 = (bf16[768,256]{1,0:T(8,128)(2,1)}, bf16[768,256]{1,0:T(8,128)(2,1)S(1)}, u32[]{:S(2)}) copy-start(bf16[768,256]{1,0:T(8,128)(2,1)S(1)} %reshape.1817) | copy-start | bytes 1179652
  201.1 9.1 %collective-permute-start = (bf16[1,80,768]{2,1,0:T(8,128)(2,1)S(1)}, bf16[1,80,768]{2,1,0:T(8,128)(2,1)S(1)}, u32[]{:S(2)}, u32[]{:S(2)}) collective-permute-start(bf16[1,80,768]{2,1,0:T(8,128)(2,1)S(1)} %fusion.285), channel_id=1, source_target_pairs={{0,16},{4,20},{8,24},{12,28},{16,0},{20,4},{24,8},{28,12},{1,17},{... | collective-permute-start | bytes 368648 | tf_op jit(solution)/shard_map/ppermute | solution.py:30
  210.3 7.3 collective-permute-start.1
  217.7 11.7 %collective-permute-start.2 = (bf16[4,80,768]{2,1,0:T(8,128)(2,1)S(1)}, bf16[4,80,768]{2,1,0:T(8,128)(2,1)S(1)}, u32[]{:S(2)}, u32[]{:S(2)}) collective-permute-start(bf16[4,80,768]{2,1,0:T(8,128)(2,1)S(1)} %pad_maximum_fusion.8), channel_id=1, source_target_pairs={{0,4},{4,0},{8,12},{12,8},{16,20},{20,16},{24,28},{28,24},{1,5},{5... | collective-permute-start | bytes 1474568 | tf_op jit(solution)/shard_map/ppermute | solution.py:30
  229.5 21.4 %collective-permute-start.3 = (bf16[8,80,768]{2,1,0:T(8,128)(2,1)S(1)}, bf16[8,80,768]{2,1,0:T(8,128)(2,1)S(1)}, u32[]{:S(2)}, u32[]{:S(2)}) collective-permute-start(bf16[8,80,768]{2,1,0:T(8,128)(2,1)S(1)} %pad_maximum_fusion.5), channel_id=1, source_target_pairs={{0,2},{1,3},{2,0},{3,1},{4,6},{5,7},{6,4},{7,5},{8,10},{9,11},{10,... | collective-permute-start | bytes 2949128 | tf_op jit(solution)/shard_map/ppermute | solution.py:30
  252.4 4.3 collective-permute-start.4
  252.4 47.0 %copy-start.138 = (s32[128]{0:T(128)}, s32[128]{0:T(128)S(1)}, u32[]{:S(2)}) copy-start(s32[128]{0:T(128)S(1)} %iota_add_fusion.1) | copy-start | bytes 1540
  266.3 33.1 %copy-start.117 = (s32[2048]{0:T(1024)}, s32[2048]{0:T(1024)S(1)}, u32[]{:S(2)}) copy-start(s32[2048]{0:T(1024)S(1)} %eq.218) | copy-start | bytes 24580
  272.7 26.7 %copy-start.9 = (f32[2048,128]{0,1:T(8,128)}, f32[2048,128]{0,1:T(8,128)S(1)}, u32[]{:S(2)}) copy-start(f32[2048,128]{0,1:T(8,128)S(1)} %get-tuple-element.387) | copy-start | bytes 3145732
  273.3 6.3 collective-permute-start.5
  279.8 3.8 collective-permute-start.6
  283.6 3.8 collective-permute-start.7
  287.5 3.8 collective-permute-start.8
  291.3 1.5 collective-permute-start.9
  300.7 3.9 collective-permute-start.10
  305.1 22.0 %collective-permute-start.11 = (bf16[8,72,768]{2,1,0:T(8,128)(2,1)S(1)}, bf16[8,72,768]{2,1,0:T(8,128)(2,1)S(1)}, u32[]{:S(2)}, u32[]{:S(2)}) collective-permute-start(bf16[8,72,768]{2,1,0:T(8,128)(2,1)S(1)} %slice.507), channel_id=1, source_target_pairs={{0,2},{1,3},{2,0},{3,1},{4,6},{5,7},{6,4},{7,5},{8,10},{9,11},{10,... | collective-permute-start | bytes 2654216 | tf_op jit(solution)/shard_map/ppermute | solution.py:30
  327.1 32.3 %slice-start.9 = ((s8[4718592]{0:T(1024)(128)(4,1)}), s8[524288]{0:T(1024)(128)(4,1)S(1)}, s32[]{:S(2)}) async-start(s8[4718592]{0:T(1024)(128)(4,1)} %bitcast.738), calls=%async_computation.11 | async-start | bytes 1048576
  327.4 26.8 %copy-start.149 = (s32[64]{0:T(128)S(1)}, s32[64]{0:T(128)}, u32[]{:S(2)}) copy-start(s32[64]{0:T(128)} %get-tuple-element.366) | copy-start | bytes 772
  327.4 11.7 %collective-permute-start.12 = (bf16[4,72,768]{2,1,0:T(8,128)(2,1)S(1)}, bf16[4,72,768]{2,1,0:T(8,128)(2,1)S(1)}, u32[]{:S(2)}, u32[]{:S(2)}) collective-permute-start(bf16[4,72,768]{2,1,0:T(8,128)(2,1)S(1)} %slice.509), channel_id=1, source_target_pairs={{0,4},{4,0},{8,12},{12,8},{16,20},{20,16},{24,28},{28,24},{1,5},{5... | collective-permute-start | bytes 1327112 | tf_op jit(solution)/shard_map/ppermute | solution.py:30
  339.2 6.1 collective-permute-start.13
  345.4 6.9 collective-permute-start.14
  536.1 36.2 %collective-permute-start.15 = (bf16[2,768,768]{2,1,0:T(8,128)(2,1)S(1)}, bf16[2,768,768]{2,1,0:T(8,128)(2,1)}, u32[]{:S(2)}, u32[]{:S(2)}) collective-permute-start(bf16[2,768,768]{2,1,0:T(8,128)(2,1)S(1)} %dynamic-slice_bitcast_fusion.24), channel_id=1, source_target_pairs={{0,1},{1,0},{2,3},{3,2},{4,5},{5,4},{6,7},{7,6},{8,9},{9,8},{10,11... | collective-permute-start | bytes 7077896 | tf_op jit(solution)/shard_map/ppermute | solution.py:30
  542.9 17.8 %collective-permute-start.28 = (bf16[2,640,768]{2,1,0:T(8,128)(2,1)}, bf16[2,640,768]{2,1,0:T(8,128)(2,1)}, u32[]{:S(2)}, u32[]{:S(2)}) collective-permute-start(bf16[2,640,768]{2,1,0:T(8,128)(2,1)} %dynamic-slice_bitcast_fusion.25), channel_id=1, source_target_pairs={{0,1},{1,0},{2,3},{3,2},{4,5},{5,4},{6,7},{7,6},{8,9},{9,8},{10,11... | collective-permute-start | bytes 5898248 | tf_op jit(solution)/shard_map/ppermute | solution.py:30
  550.6 43.1 %collective-permute-start.44 = (bf16[2,1536,768]{2,1,0:T(8,128)(2,1)}, bf16[2,1536,768]{2,1,0:T(8,128)(2,1)}, u32[]{:S(2)}, u32[]{:S(2)}) collective-permute-start(bf16[2,1536,768]{2,1,0:T(8,128)(2,1)} %dynamic-slice_bitcast_fusion.22), channel_id=1, source_target_pairs={{0,1},{1,0},{2,3},{3,2},{4,5},{5,4},{6,7},{7,6},{8,9},{9,8},{10,11... | collective-permute-start | bytes 14155784 | tf_op jit(solution)/shard_map/ppermute | solution.py:30
  560.1 17.5 %collective-permute-start.36 = (bf16[2,768,768]{2,1,0:T(8,128)(2,1)}, bf16[2,768,768]{2,1,0:T(8,128)(2,1)}, u32[]{:S(2)}, u32[]{:S(2)}) collective-permute-start(bf16[2,768,768]{2,1,0:T(8,128)(2,1)} %dynamic-slice_bitcast_fusion.23), channel_id=1, source_target_pairs={{0,1},{1,0},{2,3},{3,2},{4,5},{5,4},{6,7},{7,6},{8,9},{9,8},{10,11... | collective-permute-start | bytes 7077896 | tf_op jit(solution)/shard_map/ppermute | solution.py:30
  565.7 24.9 %collective-permute-start.29 = (bf16[1,640,768]{2,1,0:T(8,128)(2,1)}, bf16[1,640,768]{2,1,0:T(8,128)(2,1)}, u32[]{:S(2)}, u32[]{:S(2)}) collective-permute-start(bf16[1,640,768]{2,1,0:T(8,128)(2,1)} %constant_dynamic-slice_fusion.2), channel_id=1, source_target_pairs={{0,2},{1,3},{2,0},{3,1},{4,6},{5,7},{6,4},{7,5},{8,10},{9,11},{10,... | collective-permute-start | bytes 2949128 | tf_op jit(solution)/shard_map/ppermute | solution.py:30
  569.2 35.8 %collective-permute-start.23 = (f32[]{:T(128)}, f32[]{:T(128)}, u32[]{:S(2)}, u32[]{:S(2)}) collective-permute-start(f32[]{:T(128)} %sub.352), channel_id=1, source_target_pairs={{0,16},{4,20},{8,24},{12,28},{16,0},{20,4},{24,8},{28,12},{1,17},{... | collective-permute-start | bytes 20 | tf_op jit(solution)/shard_map/ppermute | solution.py:30
  576.5 123.2 %collective-permute-start.16 = (bf16[1,768,768]{2,1,0:T(8,128)(2,1)}, bf16[1,768,768]{2,1,0:T(8,128)(2,1)}, u32[]{:S(2)}, u32[]{:S(2)}) collective-permute-start(bf16[1,768,768]{2,1,0:T(8,128)(2,1)} %constant_dynamic-slice_fusion.3), channel_id=1, source_target_pairs={{0,2},{1,3},{2,0},{3,1},{4,6},{5,7},{6,4},{7,5},{8,10},{9,11},{10,... | collective-permute-start | bytes 3538952 | tf_op jit(solution)/shard_map/ppermute | solution.py:30
  581.0 121.8 %collective-permute-start.37 = (bf16[1,768,768]{2,1,0:T(8,128)(2,1)}, bf16[1,768,768]{2,1,0:T(8,128)(2,1)}, u32[]{:S(2)}, u32[]{:S(2)}) collective-permute-start(bf16[1,768,768]{2,1,0:T(8,128)(2,1)} %constant_dynamic-slice_fusion.1), channel_id=1, source_target_pairs={{0,2},{1,3},{2,0},{3,1},{4,6},{5,7},{6,4},{7,5},{8,10},{9,11},{10,... | collective-permute-start | bytes 3538952 | tf_op jit(solution)/shard_map/ppermute | solution.py:30
  592.2 105.5 %collective-permute-start.30 = (bf16[320,768]{1,0:T(8,128)(2,1)S(1)}, bf16[320,768]{1,0:T(8,128)(2,1)}, u32[]{:S(2)}, u32[]{:S(2)}) collective-permute-start(bf16[320,768]{1,0:T(8,128)(2,1)S(1)} %dynamic-slice_bitcast_fusion.30), channel_id=1, source_target_pairs={{0,4},{4,0},{8,12},{12,8},{16,20},{20,16},{24,28},{28,24},{1,5},{5... | collective-permute-start | bytes 1474568 | tf_op jit(solution)/shard_map/ppermute | solution.py:30
  600.8 114.7 %collective-permute-start.45 = (bf16[1,1536,768]{2,1,0:T(8,128)(2,1)}, bf16[1,1536,768]{2,1,0:T(8,128)(2,1)}, u32[]{:S(2)}, u32[]{:S(2)}) collective-permute-start(bf16[1,1536,768]{2,1,0:T(8,128)(2,1)} %constant_dynamic-slice_fusion), channel_id=1, source_target_pairs={{0,2},{1,3},{2,0},{3,1},{4,6},{5,7},{6,4},{7,5},{8,10},{9,11},{10,... | collective-permute-start | bytes 7077896 | tf_op jit(solution)/shard_map/ppermute | solution.py:30
  605.6 3.6 collective-permute-start.24
  609.9 3.6 collective-permute-start.25
  614.2 76.7 %collective-permute-start.26 = (f32[]{:T(128)}, f32[]{:T(128)}, u32[]{:S(2)}, u32[]{:S(2)}) collective-permute-start(f32[]{:T(128)} %add.665), channel_id=1, source_target_pairs={{0,2},{1,3},{2,0},{3,1},{4,6},{5,7},{6,4},{7,5},{8,10},{9,11},{10,... | collective-permute-start | bytes 20 | tf_op jit(solution)/shard_map/ppermute | solution.py:30
  691.5 1.2 collective-permute-start.27
  699.0 8.1 collective-permute-start.31
  701.3 22.5 %collective-permute-start.17 = (bf16[384,768]{1,0:T(8,128)(2,1)S(1)}, bf16[384,768]{1,0:T(8,128)(2,1)S(1)}, u32[]{:S(2)}, u32[]{:S(2)}) collective-permute-start(bf16[384,768]{1,0:T(8,128)(2,1)S(1)} %dynamic-slice_bitcast_fusion.29), channel_id=1, source_target_pairs={{0,4},{4,0},{8,12},{12,8},{16,20},{20,16},{24,28},{28,24},{1,5},{5... | collective-permute-start | bytes 1769480 | tf_op jit(solution)/shard_map/ppermute | solution.py:30
  707.2 8.2 collective-permute-start.32
  709.5 20.7 %collective-permute-start.38 = (bf16[384,768]{1,0:T(8,128)(2,1)S(1)}, bf16[384,768]{1,0:T(8,128)(2,1)S(1)}, u32[]{:S(2)}, u32[]{:S(2)}) collective-permute-start(bf16[384,768]{1,0:T(8,128)(2,1)S(1)} %dynamic-slice_bitcast_fusion.28), channel_id=1, source_target_pairs={{0,4},{4,0},{8,12},{12,8},{16,20},{20,16},{24,28},{28,24},{1,5},{5... | collective-permute-start | bytes 1769480 | tf_op jit(solution)/shard_map/ppermute | solution.py:30
  715.4 8.2 collective-permute-start.33
  717.9 37.6 %collective-permute-start.46 = (bf16[768,768]{1,0:T(8,128)(2,1)S(1)}, bf16[768,768]{1,0:T(8,128)(2,1)S(1)}, u32[]{:S(2)}, u32[]{:S(2)}) collective-permute-start(bf16[768,768]{1,0:T(8,128)(2,1)S(1)} %dynamic-slice_bitcast_fusion.26), channel_id=1, source_target_pairs={{0,4},{4,0},{8,12},{12,8},{16,20},{20,16},{24,28},{28,24},{1,5},{5... | collective-permute-start | bytes 3538952 | tf_op jit(solution)/shard_map/ppermute | solution.py:30
  723.7 8.9 %collective-permute-start.34 = (bf16[160,768]{1,0:T(8,128)(2,1)S(1)}, bf16[160,768]{1,0:T(8,128)(2,1)S(1)}, u32[]{:S(2)}, u32[]{:S(2)}) collective-permute-start(bf16[160,768]{1,0:T(8,128)(2,1)S(1)} %maximum_select_fusion.11), channel_id=1, source_target_pairs={{0,8},{4,12},{8,0},{12,4},{16,24},{20,28},{24,16},{28,20},{1,9},{5... | collective-permute-start | bytes 737288 | tf_op jit(solution)/shard_map/ppermute | solution.py:30
  724.0 14.5 %collective-permute-start.18 = (bf16[192,768]{1,0:T(8,128)(2,1)S(1)}, bf16[192,768]{1,0:T(8,128)(2,1)S(1)}, u32[]{:S(2)}, u32[]{:S(2)}) collective-permute-start(bf16[192,768]{1,0:T(8,128)(2,1)S(1)} %dynamic-slice_bitcast_fusion.33), channel_id=1, source_target_pairs={{0,8},{4,12},{8,0},{12,4},{16,24},{20,28},{24,16},{28,20},{1,9},{5... | collective-permute-start | bytes 884744 | tf_op jit(solution)/shard_map/ppermute | solution.py:30
  730.4 29.1 %collective-permute-start.39 = (bf16[192,768]{1,0:T(8,128)(2,1)S(1)}, bf16[192,768]{1,0:T(8,128)(2,1)S(1)}, u32[]{:S(2)}, u32[]{:S(2)}) collective-permute-start(bf16[192,768]{1,0:T(8,128)(2,1)S(1)} %dynamic-slice_bitcast_fusion.32), channel_id=1, source_target_pairs={{0,8},{4,12},{8,0},{12,4},{16,24},{20,28},{24,16},{28,20},{1,9},{5... | collective-permute-start | bytes 884744 | tf_op jit(solution)/shard_map/ppermute | solution.py:30
  732.7 68.0 %collective-permute-start.35 = (bf16[320,768]{1,0:T(8,128)(2,1)S(1)}, bf16[320,768]{1,0:T(8,128)(2,1)S(1)}, u32[]{:S(2)}, u32[]{:S(2)}) collective-permute-start(bf16[320,768]{1,0:T(8,128)(2,1)S(1)} %maximum_select_fusion.8), channel_id=1, source_target_pairs={{0,4},{4,0},{8,12},{12,8},{16,20},{20,16},{24,28},{28,24},{1,5},{5... | collective-permute-start | bytes 1474568 | tf_op jit(solution)/shard_map/ppermute | solution.py:30
  755.9 21.7 %collective-permute-start.47 = (bf16[384,768]{1,0:T(8,128)(2,1)S(1)}, bf16[384,768]{1,0:T(8,128)(2,1)S(1)}, u32[]{:S(2)}, u32[]{:S(2)}) collective-permute-start(bf16[384,768]{1,0:T(8,128)(2,1)S(1)} %dynamic-slice_bitcast_fusion.27), channel_id=1, source_target_pairs={{0,8},{4,12},{8,0},{12,4},{16,24},{20,28},{24,16},{28,20},{1,9},{5... | collective-permute-start | bytes 1769480 | tf_op jit(solution)/shard_map/ppermute | solution.py:30
  757.4 16.6 %collective-permute-start.19 = (bf16[96,768]{1,0:T(8,128)(2,1)S(1)}, bf16[96,768]{1,0:T(8,128)(2,1)S(1)}, u32[]{:S(2)}, u32[]{:S(2)}) collective-permute-start(bf16[96,768]{1,0:T(8,128)(2,1)S(1)} %dynamic-slice_bitcast_fusion.36), channel_id=1, source_target_pairs={{0,16},{4,20},{8,24},{12,28},{16,0},{20,4},{24,8},{28,12},{1,17},{... | collective-permute-start | bytes 442376 | tf_op jit(solution)/shard_map/ppermute | solution.py:30
  759.6 18.2 %collective-permute-start.40 = (bf16[96,768]{1,0:T(8,128)(2,1)S(1)}, bf16[96,768]{1,0:T(8,128)(2,1)S(1)}, u32[]{:S(2)}, u32[]{:S(2)}) collective-permute-start(bf16[96,768]{1,0:T(8,128)(2,1)S(1)} %dynamic-slice_bitcast_fusion.35), channel_id=1, source_target_pairs={{0,16},{4,20},{8,24},{12,28},{16,0},{20,4},{24,8},{28,12},{1,17},{... | collective-permute-start | bytes 442376 | tf_op jit(solution)/shard_map/ppermute | solution.py:30
  774.1 20.1 %collective-permute-start.20 = (bf16[96,768]{1,0:T(8,128)(2,1)S(1)}, bf16[96,768]{1,0:T(8,128)(2,1)S(1)}, u32[]{:S(2)}, u32[]{:S(2)}) collective-permute-start(bf16[96,768]{1,0:T(8,128)(2,1)S(1)} %fusion.238), channel_id=1, source_target_pairs={{0,16},{4,20},{8,24},{12,28},{16,0},{20,4},{24,8},{28,12},{1,17},{... | collective-permute-start | bytes 442376 | tf_op jit(solution)/shard_map/ppermute | solution.py:30
  777.8 22.8 %collective-permute-start.48 = (bf16[192,768]{1,0:T(8,128)(2,1)S(1)}, bf16[192,768]{1,0:T(8,128)(2,1)S(1)}, u32[]{:S(2)}, u32[]{:S(2)}) collective-permute-start(bf16[192,768]{1,0:T(8,128)(2,1)S(1)} %dynamic-slice_bitcast_fusion.31), channel_id=1, source_target_pairs={{0,16},{4,20},{8,24},{12,28},{16,0},{20,4},{24,8},{28,12},{1,17},{... | collective-permute-start | bytes 884744 | tf_op jit(solution)/shard_map/ppermute | solution.py:30
  777.9 32.1 %collective-permute-start.41 = (bf16[96,768]{1,0:T(8,128)(2,1)S(1)}, bf16[96,768]{1,0:T(8,128)(2,1)S(1)}, u32[]{:S(2)}, u32[]{:S(2)}) collective-permute-start(bf16[96,768]{1,0:T(8,128)(2,1)S(1)} %fusion.237), channel_id=1, source_target_pairs={{0,16},{4,20},{8,24},{12,28},{16,0},{20,4},{24,8},{28,12},{1,17},{... | collective-permute-start | bytes 442376 | tf_op jit(solution)/shard_map/ppermute | solution.py:30
  794.2 14.1 %collective-permute-start.21 = (bf16[192,768]{1,0:T(8,128)(2,1)S(1)}, bf16[192,768]{1,0:T(8,128)(2,1)S(1)}, u32[]{:S(2)}, u32[]{:S(2)}) collective-permute-start(bf16[192,768]{1,0:T(8,128)(2,1)S(1)} %maximum_select_fusion.9), channel_id=1, source_target_pairs={{0,8},{4,12},{8,0},{12,4},{16,24},{20,28},{24,16},{28,20},{1,9},{5... | collective-permute-start | bytes 884744 | tf_op jit(solution)/shard_map/ppermute | solution.py:30
  800.6 14.4 %collective-permute-start.49 = (bf16[192,768]{1,0:T(8,128)(2,1)S(1)}, bf16[192,768]{1,0:T(8,128)(2,1)S(1)}, u32[]{:S(2)}, u32[]{:S(2)}) collective-permute-start(bf16[192,768]{1,0:T(8,128)(2,1)S(1)} %fusion.218), channel_id=1, source_target_pairs={{0,16},{4,20},{8,24},{12,28},{16,0},{20,4},{24,8},{28,12},{1,17},{... | collective-permute-start | bytes 884744 | tf_op jit(solution)/shard_map/ppermute | solution.py:30
  808.5 15.3 %collective-permute-start.22 = (bf16[384,768]{1,0:T(8,128)(2,1)S(1)}, bf16[384,768]{1,0:T(8,128)(2,1)S(1)}, u32[]{:S(2)}, u32[]{:S(2)}) collective-permute-start(bf16[384,768]{1,0:T(8,128)(2,1)S(1)} %maximum_select_fusion.5), channel_id=1, source_target_pairs={{0,4},{4,0},{8,12},{12,8},{16,20},{20,16},{24,28},{28,24},{1,5},{5... | collective-permute-start | bytes 1769480 | tf_op jit(solution)/shard_map/ppermute | solution.py:30
  810.0 11.4 %collective-permute-start.42 = (bf16[192,768]{1,0:T(8,128)(2,1)S(1)}, bf16[192,768]{1,0:T(8,128)(2,1)S(1)}, u32[]{:S(2)}, u32[]{:S(2)}) collective-permute-start(bf16[192,768]{1,0:T(8,128)(2,1)S(1)} %maximum_select_fusion.10), channel_id=1, source_target_pairs={{0,8},{4,12},{8,0},{12,4},{16,24},{20,28},{24,16},{28,20},{1,9},{5... | collective-permute-start | bytes 884744 | tf_op jit(solution)/shard_map/ppermute | solution.py:30
  815.3 18.8 %collective-permute-start.50 = (bf16[384,768]{1,0:T(8,128)(2,1)S(1)}, bf16[384,768]{1,0:T(8,128)(2,1)}, u32[]{:S(2)}, u32[]{:S(2)}) collective-permute-start(bf16[384,768]{1,0:T(8,128)(2,1)S(1)} %maximum_select_fusion.7), channel_id=1, source_target_pairs={{0,8},{4,12},{8,0},{12,4},{16,24},{20,28},{24,16},{28,20},{1,9},{5... | collective-permute-start | bytes 1769480 | tf_op jit(solution)/shard_map/ppermute | solution.py:30
  821.6 17.5 %collective-permute-start.43 = (bf16[384,768]{1,0:T(8,128)(2,1)S(1)}, bf16[384,768]{1,0:T(8,128)(2,1)}, u32[]{:S(2)}, u32[]{:S(2)}) collective-permute-start(bf16[384,768]{1,0:T(8,128)(2,1)S(1)} %maximum_select_fusion.6), channel_id=1, source_target_pairs={{0,4},{4,0},{8,12},{12,8},{16,20},{20,16},{24,28},{28,24},{1,5},{5... | collective-permute-start | bytes 1769480 | tf_op jit(solution)/shard_map/ppermute | solution.py:30
  835.9 28.1 %collective-permute-start.51 = (bf16[768,768]{1,0:T(8,128)(2,1)S(1)}, bf16[768,768]{1,0:T(8,128)(2,1)}, u32[]{:S(2)}, u32[]{:S(2)}) collective-permute-start(bf16[768,768]{1,0:T(8,128)(2,1)S(1)} %maximum_select_fusion.3), channel_id=1, source_target_pairs={{0,4},{4,0},{8,12},{12,8},{16,20},{20,16},{24,28},{28,24},{1,5},{5... | collective-permute-start | bytes 3538952 | tf_op jit(solution)/shard_map/ppermute | solution.py:30
  (199 other events, 857.0 us)
Sparse Core Ops, SparseCore 0:
  23.4 58.5 all-gather.4
  83.6 73.1 all-gather.6
